TPU v7x, 512 devices: a whole 4x8x8 slice. The times are simulated.
512 devices in a mesh: tm: 32 (over y, x), pts: 16 (over z, core).
Axes of the slice: x: 4, y: 8, z: 8, core: 2. Of those that a mesh axis runs over, the one named last changes fastest.
Arguments:
- snapshots: bfloat16 [16, 512, 5, 4096], P(None, 'tm', None, 'pts'), may hold values from -8 to 8
- weights: float32 [5, 4096], P(None, 'pts'), may hold values from 1.953125e-05 to 0.0001953125
- freq_bins: int32 [256], replicated, may hold values from 0 to 255, as said below
- bin_owners: int32 [256], replicated, may hold values from 0 to 31, as said below
Outputs:
- csd: float32 [512, 512], P('tm')
Inputs may be any that keep to these rules, and one draw needn't show every extreme that they name: `freq_bins`: the listed bins are distinct. `bin_owners`: no owner holds more than 16 listed bins and one holds exactly 16; owners hold uneven numbers of bins.
All inputs are finite; a program needn't handle non-finite values.
Results may differ from a plain program's by a relative error of at most 0.00053.
Values may be sent and summed in bfloat16 or wider, within the bound.
No kernel may reach another device: no remote copies, remote signals or barrier semaphores. Data moves between devices by JAX's collectives and lax.ppermute only.
A program may use at most 64 MiB of HBM per device.

v0:
```python
import jax
import jax.numpy as jnp
from jax import lax
from jax.sharding import PartitionSpec as P

CAP = 16


def slot_index(bin_owners, owner_count):
    owner_ids = jnp.arange(owner_count, dtype=jnp.int32)
    onehot = (bin_owners[:, None] == owner_ids[None, :]).astype(jnp.int32)
    before = jnp.cumsum(onehot, axis=0) - onehot
    position = jnp.sum(before * onehot, axis=1)
    return bin_owners * CAP + position


def dft_rows(bin_values, live_mask, fft_len):
    steps_t = jnp.arange(fft_len, dtype=jnp.int32)
    wound = bin_values[:, None] * steps_t[None, :] % fft_len
    angles = 2.0 * jnp.pi * wound.astype(jnp.float32) / fft_len
    hann_window = 0.5 - 0.5 * jnp.cos(2.0 * jnp.pi * steps_t.astype(jnp.float32) / fft_len)
    scaled = hann_window / jnp.sqrt(jnp.float32(3.0 * fft_len / 8.0))
    scaled = scaled[None, :] * live_mask[:, None]
    cosine = (scaled * jnp.cos(angles)).astype(jnp.bfloat16)
    sine_rows = (-scaled * jnp.sin(angles)).astype(jnp.bfloat16)
    return jnp.stack([cosine, sine_rows], axis=1).reshape(-1, fft_len)


def fold_gram(gram_mat, blocks):
    real_part = gram_mat[..., :blocks, :blocks] + gram_mat[..., blocks:, blocks:]
    imag_part = gram_mat[..., :blocks, blocks:] - gram_mat[..., blocks:, :blocks]
    leading = gram_mat.shape[:-2]
    return jnp.concatenate(
        [
            real_part.reshape(leading + (blocks * blocks,)),
            imag_part.reshape(leading + (blocks * blocks,)),
        ],
        axis=-1,
    )


def shards(snapshots, weights, freq_bins, bin_owners):
    blocks, local_steps, fields, points = snapshots.shape
    tm_count = lax.axis_size("tm")
    fft_len = local_steps * tm_count
    sub_points = points // tm_count
    slot_count = tm_count * CAP
    by_point = lax.all_to_all(snapshots, "tm", split_axis=3, concat_axis=1, tiled=True)
    by_point = by_point.reshape(blocks, fft_len, fields * sub_points)
    slot_ids = slot_index(bin_owners, tm_count)
    matches = slot_ids[None, :] == jnp.arange(slot_count, dtype=jnp.int32)[:, None]
    is_live = jnp.any(matches, axis=1).astype(jnp.float32)
    slot_bins = jnp.sum(jnp.where(matches, freq_bins[None, :], 0), axis=1)
    dft_table = dft_rows(slot_bins, is_live, fft_len)
    spectra = jnp.einsum(
        "st,btc->sbc", dft_table, by_point, preferred_element_type=jnp.float32
    ).astype(jnp.bfloat16)
    spectra = spectra.reshape(tm_count, CAP, 2 * blocks, fields * sub_points)
    owner_weights = jnp.transpose(weights.reshape(fields, tm_count, sub_points), (1, 0, 2)).reshape(
        -1
    )
    spectra_part = lax.all_to_all(spectra, "tm", split_axis=0, concat_axis=3, tiled=True)[0]
    weighted = (spectra_part * owner_weights).astype(jnp.bfloat16)
    gram_mat = jnp.einsum(
        "kac,kbc->kab", spectra_part, weighted, preferred_element_type=jnp.float32
    )
    summed = lax.psum(gram_mat, "pts")
    return fold_gram(summed, blocks)


def solution(mesh):
    in_specs = (P(None, "tm", None, "pts"), P(None, "pts"), P(), P())
    out_specs = P("tm", None)
    return jax.shard_map(shards, mesh=mesh, in_specs=in_specs, out_specs=out_specs, check_vma=False)
```

profile of v0, /device:TPU:1, one launch (start us, length us, event | category | flops | bytes accessed | tf_op | source)
XLA Modules:
  0.0 275.1 jit_solution(10537207161755243242)
XLA Ops:
  6.5 5.1 %copy.42 = bf16[16,16,5,256]{1,0,2,3:T(8,128)(2,1)} copy(bf16[16,16,5,256]{3,1,2,0:T(8,128)(2,1)} %param.4) | data formatting | bytes 1310720 | tf_op args[0]
  11.7 0.0 copy-start
  11.7 0.0 copy-start.2
  11.7 8.4 %reshape.242 = bf16[32,2,5120]{2,1,0:T(2,128)(2,1)} reshape(bf16[256,5,16,16]{3,2,1,0:T(8,128)(2,1)} %bitcast.44) | data formatting | bytes 1310720
  20.0 10.7 %all-to-all-start = ((bf16[32,2,5120]{2,1,0:T(2,128)(2,1)}), bf16[32,2,5120]{2,1,0:T(2,128)(2,1)S(1)}, u32[]{:S(2)}, u32[]{:S(2)}) async-start(bf16[32,2,5120]{2,1,0:T(2,128)(2,1)} %reshape.242), calls=%async_computation | async-start | bytes 1310720 | tf_op jit(solution)/shard_map/all_to_all | solution.py:48
  30.7 0.0 copy-done
  30.7 0.6 reduce-window.6
  31.3 0.2 slice_reduce_fusion
  31.6 0.1 fusion.14
  31.7 0.2 fusion.11
  31.9 0.0 copy-done.2
  31.9 0.1 select_reduce_fusion
  32.1 4.8 %fusion.2 = (bf16[512,1,512]{2,0,1:T(8,128)(2,1)S(1)}, bf16[512,1,512]{2,0,1:T(8,128)(2,1)S(1)}) fusion(s32[512]{0:T(512)S(1)} %select_reduce_fusion, f32[512]{0:T(512)S(1)} %convert_element_type.67, f32[512]{0:T(512)S(1)} %subtract_multiply_fusion), kind=kLoop, calls=%fused_computation.8 | loop fusion | flops 5242880 | bytes 1054720 | tf_op jit(solution)/shard_map/convert_element_type | solution.py:24
  36.9 0.1 pad_maximum_fusion
  37.0 1.1 copy.41
  38.1 0.4 reshape.233
  38.5 10.7 %all-to-all-done = bf16[32,2,5120]{2,1,0:T(2,128)(2,1)S(1)} async-done(((bf16[32,2,5120]{2,1,0:T(2,128)(2,1)}), bf16[32,2,5120]{2,1,0:T(2,128)(2,1)S(1)}, u32[]{:S(2)}, u32[]{:S(2)}) %all-to-all-start) | async-done | bytes 655392 | tf_op jit(solution)/shard_map/all_to_all | solution.py:48
  49.2 4.9 %reshape.243 = bf16[256,5,16,16]{3,2,1,0:T(8,128)(2,1)} reshape(bf16[32,2,5120]{2,1,0:T(2,128)(2,1)S(1)} %all-to-all-done) | data formatting | bytes 1310720
  54.2 8.2 %copy.44 = bf16[16,32,16,5,8]{2,1,4,3,0:T(8,128)(2,1)} copy(bf16[16,32,16,5,8]{2,0,3,4,1:T(8,128)(2,1)} %bitcast.43) | data formatting | bytes 1310720 | tf_op jit(solution)/shard_map/all_to_all | solution.py:48
  62.4 9.4 %reshape.234 = bf16[16,512,40]{1,2,0:T(8,128)(2,1)S(1)} reshape(bf16[16,32,16,5,8]{2,1,4,3,0:T(8,128)(2,1)} %copy.44) | data formatting | bytes 1310720 | tf_op jit(solution)/shard_map/reshape | solution.py:49
  71.8 0.9 fusion.16
  72.7 0.2 convert_element_type.71
  72.9 4.8 %copy.45 = bf16[1024,16,40]{2,1,0:T(8,128)(2,1)} copy(bf16[1024,16,40]{0,2,1:T(8,128)(2,1)S(1)} %convert_element_type.71) | data formatting | bytes 2621440 | tf_op jit(solution)/shard_map/convert_element_type | solution.py:57
  77.7 9.6 %reshape.244 = bf16[32,2,10240]{2,1,0:T(2,128)(2,1)} reshape(bf16[32,16,32,40]{3,2,1,0:T(8,128)(2,1)} %bitcast.46) | data formatting | bytes 2621440
  87.3 0.0 copy-start.1
  87.3 5.7 %all-to-all-start.1 = ((bf16[32,2,10240]{2,1,0:T(2,128)(2,1)}), bf16[32,2,10240]{2,1,0:T(2,128)(2,1)S(1)}, u32[]{:S(2)}, u32[]{:S(2)}) async-start(bf16[32,2,10240]{2,1,0:T(2,128)(2,1)} %reshape.244), calls=%async_computation.1 | async-start | bytes 2621440 | tf_op jit(solution)/shard_map/all_to_all | solution.py:62
  93.0 0.0 all-reduce.2.cloned.1.call-start
  93.0 0.0 copy-done.1
  93.0 0.1 reshape.236
  93.2 0.1 copy.47
  93.2 0.1 mul.111
  93.3 30.5 %all-to-all-done.1 = bf16[32,2,10240]{2,1,0:T(2,128)(2,1)S(1)} async-done(((bf16[32,2,10240]{2,1,0:T(2,128)(2,1)}), bf16[32,2,10240]{2,1,0:T(2,128)(2,1)S(1)}, u32[]{:S(2)}, u32[]{:S(2)}) %all-to-all-start.1) | async-done | bytes 1310752 | tf_op jit(solution)/shard_map/all_to_all | solution.py:62
  123.9 7.6 %reshape.245 = bf16[32,16,32,40]{3,2,1,0:T(8,128)(2,1)} reshape(bf16[32,2,10240]{2,1,0:T(2,128)(2,1)S(1)} %all-to-all-done.1) | data formatting | bytes 2621440
  131.4 6.9 %copy.46 = bf16[1,16,32,32,40]{4,3,2,1,0:T(8,128)(2,1)} copy(bf16[1,16,32,32,40]{4,2,1,3,0:T(8,128)(2,1)} %bitcast.47) | data formatting | bytes 2621440 | tf_op jit(solution)/shard_map/all_to_all | solution.py:62
  138.3 6.9 %squeeze.3 = bf16[16,32,1280]{2,1,0:T(8,128)(2,1)S(1)} reshape(bf16[1,16,32,32,40]{4,3,2,1,0:T(8,128)(2,1)} %copy.46) | data formatting | bytes 2621440 | tf_op jit(solution)/shard_map/squeeze | solution.py:62
  145.1 1.2 fusion
  146.3 0.0 all-reduce.2.cloned.1.call-update
  146.4 119.8 %all-reduce.2.cloned.1.call-done = f32[16,32,32]{2,1,0:T(8,128)} async-done(((f32[16,32,32]{2,1,0:T(8,128)}), f32[16,32,32]{2,1,0:T(8,128)}) %all-reduce.2.cloned.1.call-update) | async-done | bytes 65552 | tf_op jit(solution)/shard_map/psum | solution.py:67
  266.1 1.2 slice_add_fusion
  267.4 0.1 reshape.237
  267.5 0.1 reshape.238
  267.6 0.6 pad_maximum_fusion.1
  (6 shorter events, 0.1 us)
Async XLA Ops:
  11.7 19.0 %copy-start = (s32[256]{0:T(256)S(1)}, s32[256]{0:T(256)}, u32[]{:S(2)}) copy-start(s32[256]{0:T(256)} %param.7) | copy-start | bytes 3076
  11.7 20.2 %copy-start.2 = (s32[256]{0:T(256)S(1)}, s32[256]{0:T(256)}, u32[]{:S(2)}) copy-start(s32[256]{0:T(256)} %param.6) | copy-start | bytes 3076
  20.0 29.2 %all-to-all-start = ((bf16[32,2,5120]{2,1,0:T(2,128)(2,1)}), bf16[32,2,5120]{2,1,0:T(2,128)(2,1)S(1)}, u32[]{:S(2)}, u32[]{:S(2)}) async-start(bf16[32,2,5120]{2,1,0:T(2,128)(2,1)} %reshape.242), calls=%async_computation | async-start | bytes 1310720 | tf_op jit(solution)/shard_map/all_to_all | solution.py:48
  87.3 5.7 %copy-start.1 = (f32[5,256]{1,0:T(8,128)S(1)}, f32[5,256]{1,0:T(8,128)}, u32[]{:S(2)}) copy-start(f32[5,256]{1,0:T(8,128)} %param.5) | copy-start | bytes 15364
  87.3 36.5 %all-to-all-start.1 = ((bf16[32,2,10240]{2,1,0:T(2,128)(2,1)}), bf16[32,2,10240]{2,1,0:T(2,128)(2,1)S(1)}, u32[]{:S(2)}, u32[]{:S(2)}) async-start(bf16[32,2,10240]{2,1,0:T(2,128)(2,1)} %reshape.244), calls=%async_computation.1 | async-start | bytes 2621440 | tf_op jit(solution)/shard_map/all_to_all | solution.py:62
  93.0 173.1 %all-reduce.2.cloned.1.call-start = ((), (), s32[]{:S(2)}) async-start(), calls=%async_computation.2 | async-start | bytes 524288 | tf_op jit(solution)/shard_map/psum | solution.py:67
Sparse Core Ops, SparseCore 0:
  146.5 119.6 all-reduce.1
where the time goes:
time: 276 us; the launch traced here: 275 us
  waiting for transfers between devices  161 us (58%)
  local copies, waits for them, and re-layouts  74 us (27%)
  starting transfers between devices  16.4 us (6%)
  between operations  13.6 us (5%)
  other arithmetic  8.05 us (3%)
    psum x1, waiting for transfers between devices, shards(): summed = lax.psum(gram_mat, 'pts')  120 us
    unnamed x11, local copies, waits for them, and re-layouts  35.6 us
    all_to_all x1, waiting for transfers between devices, shards(): lax.all_to_all(spectra, 'tm', split_axis=0, concat_axis=3, tiled=True)[0]  30.5 us
    all_to_all x1, waiting for transfers between devices, shards(): lax.all_to_all(snapshots, 'tm', split_axis=3, concat_axis=1, tiled=True)  10.7 us
    all_to_all x1, starting transfers between devices, shards(): lax.all_to_all(snapshots, 'tm', split_axis=3, concat_axis=1, tiled=True)  10.7 us
    reshape x1, local copies, waits for them, and re-layouts, shards(): by_point = by_point.reshape(blocks, fft_len, fields * sub_points)  9.41 us
    all_to_all x1, local copies, waits for them, and re-layouts, shards(): lax.all_to_all(snapshots, 'tm', split_axis=3, concat_axis=1, tiled=True)  8.21 us
    all_to_all x1, local copies, waits for them, and re-layouts, shards(): lax.all_to_all(spectra, 'tm', split_axis=0, concat_axis=3, tiled=True)[0]  6.86 us
  transfers between devices with their start and end apart: 3, of which 3 were waited for; matrix products, arithmetic and copies ran while one was open for 3% of the time, Pallas kernels for 0%

commit v1 on v0

v1 whole, which is shorter than its diff:
```python
import functools

import jax
import jax.numpy as jnp
import numpy as np
from jax import lax
from jax.experimental import pallas as pl
from jax.experimental.pallas import tpu as pltpu
from jax.sharding import PartitionSpec as P

CAP = 16
LANES = 128


def dft_rows(bin_values, fft_len):
    steps_t = jnp.arange(fft_len, dtype=jnp.int32)
    wound = bin_values[:, None] * steps_t[None, :] % fft_len
    angles = 2.0 * jnp.pi * wound.astype(jnp.float32) / fft_len
    hann_window = 0.5 - 0.5 * jnp.cos(2.0 * jnp.pi * steps_t.astype(jnp.float32) / fft_len)
    scaled = hann_window / jnp.sqrt(jnp.float32(3.0 * fft_len / 8.0))
    cosine = (scaled * jnp.cos(angles)).astype(jnp.bfloat16)
    sine_rows = (-scaled * jnp.sin(angles)).astype(jnp.bfloat16)
    return jnp.concatenate([cosine, sine_rows], axis=0)


def slot_rows(bin_owners, slot_count):
    count = bin_owners.shape[0]
    listed = jnp.arange(count, dtype=jnp.int32)
    same = (bin_owners[:, None] == bin_owners[None, :]) & (listed[None, :] < listed[:, None])
    position = jnp.sum(same.astype(jnp.int32), axis=1)
    slots = bin_owners * CAP + position
    return (jnp.arange(slot_count, dtype=jnp.int32)[:, None] == slots[None, :]).astype(jnp.bfloat16)


def scatter_body(x_ref, out_ref):
    blocks, fields = x_ref.shape[0], x_ref.shape[1]
    group = lax.broadcasted_iota(jnp.int32, x_ref.shape[2:], 1) // (LANES // blocks)
    width = LANES // blocks
    for f in range(fields):
        rows = []
        for b in range(blocks):
            row = x_ref[b, f].astype(jnp.float32)
            rows.append(pltpu.roll(row, width * b, 1) if b else row)
        bit = 1
        while bit < blocks:
            take = (group & bit) != 0
            rows = [jnp.where(take, rows[(c + bit) % blocks], rows[c]) for c in range(blocks)]
            bit *= 2
        for d in range(blocks):
            row = rows[(blocks - d) % blocks]
            if d:
                row = pltpu.roll(row, LANES - width * d, 1)
            out_ref[d, f] = row.astype(jnp.bfloat16)


def scatter_points(x):
    blocks, fields, steps, points = x.shape
    tiles = points // LANES
    return pl.pallas_call(
        scatter_body,
        grid=(tiles,),
        out_shape=jax.ShapeDtypeStruct((blocks * tiles, fields, steps, LANES), jnp.bfloat16),
        in_specs=[pl.BlockSpec((blocks, fields, steps, LANES), lambda h: (0, 0, 0, h))],
        out_specs=pl.BlockSpec((blocks, fields, steps, LANES), lambda h: (h, 0, 0, 0)),
        name="scatter_points",
    )(x)


def split2(value):
    high = value.astype(jnp.bfloat16)
    return high, (value - high.astype(jnp.float32)).astype(jnp.bfloat16)


def gram_body(x_ref, table_ref, w_ref, pick_ref, slot_ref, out_ref, spec, high, low):
    fields = x_ref.shape[1]
    steps = x_ref.shape[0] * x_ref.shape[2]
    count = table_ref.shape[0] // 2
    for f in range(fields):
        part = jnp.dot(
            table_ref[...],
            x_ref[:, f].reshape(steps, LANES),
            preferred_element_type=jnp.float32,
        )
        spec[f] = part.astype(jnp.bfloat16).astype(jnp.float32)
    rows = 16
    left = lax.broadcasted_iota(jnp.int32, (rows, LANES), 1) < LANES // 2

    def chunk(c, carry):
        at = pl.multiple_of(c * rows, rows)
        re = [spec[f, pl.ds(at, rows), :] for f in range(fields)]
        im = [spec[f, pl.ds(count + at, rows), :] for f in range(fields)]
        wre = [re[f] * w_ref[f : f + 1, :] for f in range(fields)]
        wim = [im[f] * w_ref[f : f + 1, :] for f in range(fields)]

        def put(j, value):
            hi, lo = split2(value)
            high[pl.ds(at, rows), j * LANES : (j + 1) * LANES] = hi
            low[pl.ds(at, rows), j * LANES : (j + 1) * LANES] = lo

        for delta in range(9):
            if delta:
                qre = [pltpu.roll(v, LANES - 8 * delta, 1) for v in wre]
                qim = [pltpu.roll(v, LANES - 8 * delta, 1) for v in wim]
            else:
                qre, qim = wre, wim
            real = sum(re[f] * qre[f] + im[f] * qim[f] for f in range(fields))
            if delta == 0:
                put(0, real)
                continue
            imag = sum(re[f] * qim[f] - im[f] * qre[f] for f in range(fields))
            if delta < 8:
                put(delta, real)
                put(delta + 7, imag)
            else:
                put(15, jnp.where(left, real, pltpu.roll(imag, LANES // 2, 1)))
        return carry

    lax.fori_loop(0, count // rows, chunk, 0)
    packed = jnp.dot(high[...], pick_ref[...], preferred_element_type=jnp.float32) + jnp.dot(
        low[...], pick_ref[...], preferred_element_type=jnp.float32
    )
    hi, lo = split2(packed)
    out_ref[...] = jnp.dot(slot_ref[...], hi, preferred_element_type=jnp.float32) + jnp.dot(
        slot_ref[...], lo, preferred_element_type=jnp.float32
    )


def gram_sums(by_point, table, lane_weights, pick, slots):
    fields = by_point.shape[1]
    count = table.shape[0] // 2
    wide = 16 * LANES
    return pl.pallas_call(
        gram_body,
        out_shape=jax.ShapeDtypeStruct((slots.shape[0], 256), jnp.float32),
        scratch_shapes=[
            pltpu.VMEM((fields, 2 * count, LANES), jnp.float32),
            pltpu.VMEM((count, wide), jnp.bfloat16),
            pltpu.VMEM((count, wide), jnp.bfloat16),
        ],
        name="gram_sums",
    )(by_point, table, lane_weights, pick, slots)


def unpack_matrix(blocks):
    table = np.zeros((256, 2 * blocks * blocks), np.float32)
    half = blocks // 2
    for b in range(blocks):
        for e in range(blocks):
            delta = (e - b) % blocks
            if delta < half:
                real, imag, sign = 16 * delta + b, 16 * (delta + 7) + b, 1.0
            elif delta == half:
                real, imag, sign = 240 + b % half, 248 + b % half, 1.0 if b < half else -1.0
            else:
                back = blocks - delta
                real, imag, sign = 16 * back + e, 16 * (back + 7) + e, -1.0
            table[real, b * blocks + e] = 1.0
            if delta:
                table[imag, blocks * blocks + b * blocks + e] = sign
    return table


def shards(snapshots, weights, freq_bins, bin_owners):
    blocks, local_steps, fields, points = snapshots.shape
    tm_count = lax.axis_size("tm")
    pts_count = lax.axis_size("pts")
    fft_len = local_steps * tm_count
    sub_points = points // tm_count
    slot_count = tm_count * CAP
    sent = scatter_points(jnp.transpose(snapshots, (0, 2, 1, 3)))
    by_point = lax.all_to_all(sent, "tm", split_axis=0, concat_axis=0, tiled=True)
    table = dft_rows(freq_bins, fft_len)
    slots = slot_rows(bin_owners, slot_count)
    mine = lax.dynamic_slice(weights, (0, lax.axis_index("tm") * sub_points), (fields, sub_points))
    lane_weights = jnp.tile(mine, (1, blocks))
    pick = (
        jnp.arange(16 * LANES, dtype=jnp.int32)[:, None] // 8
        == jnp.arange(256, dtype=jnp.int32)[None, :]
    ).astype(jnp.bfloat16)
    partial = gram_sums(by_point, table, lane_weights, pick, slots)
    partial = partial.reshape(tm_count, CAP, 256)
    owned = jnp.sum(lax.all_to_all(partial, "tm", split_axis=0, concat_axis=0, tiled=True), axis=0)
    row = jnp.sum(lax.all_to_all(owned, "pts", split_axis=0, concat_axis=0, tiled=True), axis=0)
    rows = jnp.broadcast_to(row[None, :], (pts_count, 256))
    summed = lax.all_to_all(rows, "pts", split_axis=0, concat_axis=0, tiled=True)
    return jnp.dot(
        summed, jnp.asarray(unpack_matrix(blocks)), precision=lax.Precision.HIGHEST
    )


def solution(mesh):
    in_specs = (P(None, "tm", None, "pts"), P(None, "pts"), P(), P())
    out_specs = P("tm", None)
    return jax.shard_map(shards, mesh=mesh, in_specs=in_specs, out_specs=out_specs, check_vma=False)
```

time: 276 us -> 96 us (0.35)
  waiting for transfers between devices: 161 us -> 12.2 us
  local copies, waits for them, and re-layouts: 74 us -> 1.66 us
  blocking collectives: 0 us -> 52.1 us
  between operations: 13.6 us -> 0.07 us
  Pallas kernels: 0 us -> 12.2 us
  starting transfers between devices: 16.4 us -> 10.6 us
    psum x1 -> x0, waiting for transfers between devices: 120 us -> none  [shards(): summed = lax.psum(gram_mat, 'pts')]
    all_to_all x0 -> x3, blocking collectives: none -> 52.1 us  [the longest x1 21.1 us: shards(): lax.all_to_all(owned, 'pts', split_axis=0, concat_axis=0, tiled=True)]
    unnamed x11 -> x10, local copies, waits for them, and re-layouts: 35.6 us -> 0.87 us
    all_to_all x2 -> x1, waiting for transfers between devices: 41.2 us -> 12.2 us  [shards(): lax.all_to_all(sent, 'tm', split_axis=0, concat_axis=0, tiled=True)]
    all_to_all x2 -> x1, local copies, waits for them, and re-layouts: 15.1 us -> 0.01 us  [shards(): lax.all_to_all(owned, 'pts', split_axis=0, concat_axis=0, tiled=True)]
    pallas_call x0 -> x2, Pallas kernels: none -> 12.2 us  [the longest x1 9.44 us: gram_sums(): pl.pallas_call(gram_body, out_shape=jax.ShapeDtypeStruct((slots.shape[0],...]
    reshape x5 -> x0, local copies, waits for them, and re-layouts: 10.2 us -> none  [the longest x1 9.41 us: shards(): by_point = by_point.reshape(blocks, fft_len, fields * sub_points)]
    squeeze x1 -> x0, local copies, waits for them, and re-layouts: 6.85 us -> none  [shards(): lax.all_to_all(spectra, 'tm', split_axis=0, concat_axis=3, tiled=True)[0]]
  transfers between devices with their start and end apart: 3 -> 1, of which waited for: 3 -> 1; matrix products, arithmetic and copies ran while one was open for 3% -> 7% of each run, Pallas kernels for 0% -> 0%
where the time goes in v1:
time: 96 us; the launch traced here: 95.5 us
  blocking collectives  52.1 us (54%)
  Pallas kernels  12.2 us (13%)
  waiting for transfers between devices  12.2 us (13%)
  starting transfers between devices  10.6 us (11%)
  other arithmetic  5.7 us (6%)
  local copies, waits for them, and re-layouts  1.66 us (2%)
  matrix products  0.99 us (1%)
    all_to_all x1, blocking collectives, shards(): lax.all_to_all(owned, 'pts', split_axis=0, concat_axis=0, tiled=True)  21.1 us
    all_to_all x1, blocking collectives, shards(): lax.all_to_all(partial, 'tm', split_axis=0, concat_axis=0, tiled=True)  20.8 us
    all_to_all x1, waiting for transfers between devices, shards(): lax.all_to_all(sent, 'tm', split_axis=0, concat_axis=0, tiled=True)  12.2 us
    all_to_all x1, starting transfers between devices, shards(): lax.all_to_all(sent, 'tm', split_axis=0, concat_axis=0, tiled=True)  10.6 us
    all_to_all x1, blocking collectives, shards(): lax.all_to_all(rows, 'pts', split_axis=0, concat_axis=0, tiled=True)  10.2 us
    pallas_call x1, Pallas kernels, gram_sums(): pl.pallas_call(gram_body, out_shape=jax.ShapeDtypeStruct((slots.shape[0],...  9.44 us
    pallas_call x1, Pallas kernels, scatter_points(): pl.pallas_call(scatter_body, grid=(tiles,), out_shape=jax.ShapeDtypeStruc...  2.73 us
    convert_element_type x1, other arithmetic, dft_rows(): cosine = (scaled * jnp.cos(angles)).astype(jnp.bfloat16)  2.46 us
  transfers between devices with their start and end apart: 1, of which 1 were waited for; matrix products, arithmetic and copies ran while one was open for 7% of the time, Pallas kernels for 0%

profile of v1, /device:TPU:1, one launch (start us, length us, event | category | flops | bytes accessed | tf_op | source)
XLA Modules:
  0.0 95.5 jit_solution(6118730440103294838)
XLA Ops:
  0.0 0.0 copy-start
  0.0 0.0 copy-start.3
  0.0 2.7 %scatter_points.1 = bf16[32,5,16,128]{3,2,1,0:T(8,128)(2,1)} custom-call(bf16[16,5,16,256]{3,2,1,0:T(8,128)(2,1)} %bitcast.7), custom_call_target="tpu_custom_call" | custom-call | tf_op jit(solution)/shard_map/scatter_points/pallas_call | solution.py:59
  2.7 0.0 copy-start.4
  2.7 10.6 %all-to-all-start = ((bf16[32,5,16,128]{3,2,1,0:T(8,128)(2,1)}), bf16[32,5,16,128]{3,2,1,0:T(8,128)(2,1)S(1)}, u32[]{:S(2)}, u32[]{:S(2)}) async-start(bf16[32,5,16,128]{3,2,1,0:T(8,128)(2,1)} %scatter_points.1), calls=%async_computation | async-start | bytes 1310720 | tf_op jit(solution)/shard_map/all_to_all | solution.py:171
  13.4 0.0 copy-done.3
  13.4 0.2 convert_reduce_fusion
  13.6 0.0 copy-done
  13.6 0.1 constant_dynamic-slice_fusion
  13.7 0.7 tile.10.w_ref
  14.4 0.0 copy-done.4
  14.4 2.5 %multiply_convert_fusion.1 = (bf16[256,512]{1,0:T(8,128)(2,1)S(1)}, bf16[256,512]{1,0:T(8,128)(2,1)S(1)}) fusion(s32[256]{0:T(256)S(1)} %copy-done.4, f32[512]{0:T(512)S(1)} %get-tuple-element.7, f32[512]{0:T(512)S(1)} %get-tuple-element.8), kind=kLoop, calls=%fused_computation.11 | loop fusion | flops 2359296 | bytes 529408 | tf_op jit(solution)/shard_map/convert_element_type | solution.py:21
  16.9 0.8 pad_maximum_fusion.table_ref
  17.7 0.8 fusion.7.slot_ref
  18.5 1.3 %fusion.pick_ref = bf16[2048,256]{1,0:T(8,128)(2,1)} fusion(s32[2048]{0:T(1024)S(1)} %add_select_fusion.1), kind=kLoop, calls=%fused_computation.1 | loop fusion | flops 1048576 | bytes 1056768 | tf_op jit(solution)/shard_map/convert_element_type | solution.py:179
  19.8 12.2 %all-to-all-done.x_ref = bf16[32,5,16,128]{3,2,1,0:T(8,128)(2,1)S(1)} async-done(((bf16[32,5,16,128]{3,2,1,0:T(8,128)(2,1)}), bf16[32,5,16,128]{3,2,1,0:T(8,128)(2,1)S(1)}, u32[]{:S(2)}, u32[]{:S(2)}) %all-to-all-start) | async-done | bytes 655392 | tf_op jit(solution)/shard_map/all_to_all | solution.py:171
  32.1 0.0 copy-start.1
  32.1 0.8 copy-done.1
  32.9 9.4 %gram_sums.1 = f32[512,256]{1,0:T(8,128)} custom-call(bf16[32,5,16,128]{3,2,1,0:T(8,128)(2,1)} %copy-done.1, bf16[512,512]{1,0:T(8,128)(2,1)} %pad_maximum_fusion.table_ref, f32[5,128]{1,0:T(8,128)} %tile.10.w_ref, bf16[2048,256]{1,0:T(8,128)(2,1)} %fusion.pick_ref, bf16[512,256]{1,0:T(8,128)(2,1)} %fusion.7.slot_ref), custom_call_target="tpu_custom_call" | custom-call | tf_op jit(solution)/shard_map/gram_sums/pallas_call | solution.py:132
  42.3 0.0 copy-start.2
  42.3 20.8 %all_to_all.28 = f32[32,16,256]{2,1,0:T(8,128)S(1)} all-to-all(f32[32,16,256]{2,1,0:T(8,128)} %bitcast.6), channel_id=1, replica_groups=mesh['tm'=32,'pts'=16] {'tm'}, dimensions={0} | all-to-all | bytes 1048576 | tf_op jit(solution)/shard_map/all_to_all | solution.py:182
  63.2 21.1 %all_to_all.29 = f32[16,1,256]{2,1,0:T(1,128)S(1)} all-to-all(f32[16,1,256]{2,1,0:T(1,128)S(1)} %all_to_all.20), channel_id=1, replica_groups=mesh['tm'=32,'pts'=16] {'pts'}, dimensions={0} | all-to-all | bytes 32768 | tf_op jit(solution)/shard_map/all_to_all | solution.py:183
  84.4 10.2 %all_to_all.30 = f32[16,1,256]{2,1,0:T(1,128)S(1)} all-to-all(f32[16,1,256]{2,1,0:T(1,128)S(1)} %broadcast_in_dim.2), channel_id=1, replica_groups=mesh['tm'=32,'pts'=16] {'pts'}, dimensions={0} | all-to-all | bytes 32768 | tf_op jit(solution)/shard_map/all_to_all | solution.py:185
  94.6 0.0 copy-done.2
  94.6 1.0 %fusion.9 = f32[16,512]{1,0:T(8,128)} fusion(f32[256,512]{1,0:T(8,128)S(1)} %copy-done.2, f32[16,1,256]{2,1,0:T(1,128)S(1)} %all_to_all.30), kind=kOutput, calls=%fused_computation.23 | convolution fusion | flops 25165824 | bytes 573440 | tf_op jit(solution)/shard_map/dot_general | solution.py:186
  (8 shorter events, 0.2 us)
Async XLA Ops:
  0.0 13.6 %copy-start = (f32[5,256]{1,0:T(8,128)S(1)}, f32[5,256]{1,0:T(8,128)}, u32[]{:S(2)}) copy-start(f32[5,256]{1,0:T(8,128)} %param.6) | copy-start | bytes 15364
  0.0 13.4 %copy-start.3 = (s32[256]{0:T(256)S(1)}, s32[256]{0:T(256)}, u32[]{:S(2)}) copy-start(s32[256]{0:T(256)} %param.8) | copy-start | bytes 3076
  2.7 11.7 %copy-start.4 = (s32[256]{0:T(256)S(1)}, s32[256]{0:T(256)}, u32[]{:S(2)}) copy-start(s32[256]{0:T(256)} %param.7) | copy-start | bytes 3076
  2.7 29.3 %all-to-all-start = ((bf16[32,5,16,128]{3,2,1,0:T(8,128)(2,1)}), bf16[32,5,16,128]{3,2,1,0:T(8,128)(2,1)S(1)}, u32[]{:S(2)}, u32[]{:S(2)}) async-start(bf16[32,5,16,128]{3,2,1,0:T(8,128)(2,1)} %scatter_points.1), calls=%async_computation | async-start | bytes 1310720 | tf_op jit(solution)/shard_map/all_to_all | solution.py:171
  32.1 0.9 copy-start.1
  42.3 52.2 %copy-start.2 = (f32[256,512]{1,0:T(8,128)S(1)}, f32[256,512]{1,0:T(8,128)}, u32[]{:S(2)}) copy-start(f32[256,512]{1,0:T(8,128)} %constant.63.clone) | copy-start | bytes 1572868

commit v2 on v1

v2 whole, which is shorter than its diff:
```python
import functools

import jax
import jax.numpy as jnp
import numpy as np
from jax import lax
from jax.experimental import pallas as pl
from jax.experimental.pallas import tpu as pltpu
from jax.sharding import PartitionSpec as P

CAP = 16
LANES = 128


def dft_columns(bin_values, fft_len):
    steps_t = jnp.arange(fft_len, dtype=jnp.int32)[:, None]
    wound = bin_values[None, :] * steps_t % fft_len
    angles = 2.0 * jnp.pi * wound.astype(jnp.float32) / fft_len
    hann_window = 0.5 - 0.5 * jnp.cos(2.0 * jnp.pi * steps_t.astype(jnp.float32) / fft_len)
    scaled = hann_window / jnp.sqrt(jnp.float32(3.0 * fft_len / 8.0))
    cosine = (scaled * jnp.cos(angles)).astype(jnp.bfloat16)
    sine_rows = (-scaled * jnp.sin(angles)).astype(jnp.bfloat16)
    return jnp.concatenate([cosine, sine_rows], axis=1)


def slot_rows(bin_owners, slot_count):
    count = bin_owners.shape[0]
    listed = jnp.arange(count, dtype=jnp.int32)
    same = (bin_owners[:, None] == bin_owners[None, :]) & (listed[None, :] < listed[:, None])
    position = jnp.sum(same.astype(jnp.int32), axis=1)
    slots = bin_owners * CAP + position
    return (jnp.arange(slot_count, dtype=jnp.int32)[:, None] == slots[None, :]).astype(jnp.bfloat16)


def scatter_body(x_ref, out_ref):
    blocks, fields, steps = x_ref.shape[:3]
    groups = 16
    width = LANES // groups
    group = lax.broadcasted_iota(jnp.int32, (steps, LANES), 1) // width
    sources = []
    for pair in range(fields // 2):
        for first in range(0, blocks, groups // 2):
            sources.append([(first + g // 2, 2 * pair + g % 2) for g in range(groups)])
    sources.append([(g, fields - 1) for g in range(groups)])
    for tile, source in enumerate(sources):
        rows = []
        for g, (b, f) in enumerate(source):
            row = x_ref[b, f].astype(jnp.float32)
            rows.append(pltpu.roll(row, width * g, 1) if g else row)
        bit = 1
        while bit < groups:
            take = (group & bit) != 0
            rows = [jnp.where(take, rows[(c + bit) % groups], rows[c]) for c in range(groups)]
            bit *= 2
        for d in range(groups):
            row = rows[(groups - d) % groups]
            if d:
                row = pltpu.roll(row, LANES - width * d, 1)
            out_ref[d, :, tile * LANES : (tile + 1) * LANES] = row.astype(jnp.bfloat16)


def scatter_points(x):
    blocks, fields, steps, points = x.shape
    tiles = points // LANES
    wide = fields * blocks * points // (16 * tiles)
    return pl.pallas_call(
        scatter_body,
        grid=(tiles,),
        out_shape=jax.ShapeDtypeStruct((16 * tiles, steps, wide), jnp.bfloat16),
        in_specs=[pl.BlockSpec((blocks, fields, steps, LANES), lambda h: (0, 0, 0, h))],
        out_specs=pl.BlockSpec((16, steps, wide), lambda h: (h, 0, 0)),
        name="scatter_points",
    )(x)


def gram_body(x_ref, table_ref, w_ref, slot_ref, out_ref, plain, weighted, sums, packed):
    steps = x_ref.shape[0] * x_ref.shape[1]
    count = table_ref.shape[1] // 2
    wide = x_ref.shape[2]
    tiles = wide // LANES
    for tile in range(tiles):
        cols = slice(tile * LANES, (tile + 1) * LANES)
        spec = lax.dot_general(
            x_ref[:, :, cols].reshape(steps, LANES),
            table_ref[...],
            (((0,), (0,)), ((), ())),
            preferred_element_type=jnp.float32,
        )
        spec = spec.astype(jnp.bfloat16).astype(jnp.float32)
        row_w = w_ref[cols, :]
        scaled = spec * jnp.concatenate([row_w] * (2 * count // LANES), axis=1)
        if tile < tiles - 1:
            half, at = tile // 2, tile % 2 * LANES
            plain[half, at : at + LANES, :] = spec.astype(jnp.bfloat16)
            scaled = scaled.astype(jnp.bfloat16)
            weighted[half, at : at + LANES, :] = scaled
            if at == 0:
                weighted[half, 2 * LANES :, :] = scaled
        else:
            half = tiles // 2
            gap = jnp.zeros((16, 8, 2 * count), jnp.float32)
            for ref, value in ((plain, spec), (weighted, scaled)):
                value = jnp.concatenate([value.reshape(16, 8, 2 * count), gap], axis=1)
                value = value.reshape(2 * LANES, 2 * count).astype(jnp.bfloat16)
                ref[half, : 2 * LANES, :] = value
                if ref is weighted:
                    ref[half, 2 * LANES :, :] = value[:LANES]
    halves = plain.shape[0]

    def block(b, last):
        at = pl.multiple_of(b * 16, 16)
        re = [plain[h, pl.ds(at, 16), :count] for h in range(halves)]
        im = [plain[h, pl.ds(at, 16), count:] for h in range(halves)]
        for delta in range(last + 1):
            to = pl.multiple_of(at + delta * 16, 16)
            qre = [weighted[h, pl.ds(to, 16), :count] for h in range(halves)]
            qim = [weighted[h, pl.ds(to, 16), count:] for h in range(halves)]
            real = sum(re[h] * qre[h] + im[h] * qim[h] for h in range(halves))
            where = delta if delta < 8 else 15
            sums[pl.ds(pl.multiple_of(where * 256 + at, 16), 16), :] = real
            if delta:
                imag = sum(re[h] * qim[h] - im[h] * qre[h] for h in range(halves))
                offset = (delta + 7) * 256 if delta < 8 else 15 * 256 + 128
                sums[pl.ds(pl.multiple_of(offset + at, 16), 16), :] = imag

    lax.fori_loop(0, 8, lambda b, carry: (block(b, 8), carry)[1], 0)
    lax.fori_loop(8, 16, lambda b, carry: (block(b, 7), carry)[1], 0)
    sel = lax.broadcasted_iota(jnp.int32, (16, 256), 1) // 16
    sel = (sel == lax.broadcasted_iota(jnp.int32, (16, 256), 0)).astype(jnp.bfloat16)
    for j in range(16):
        part = jnp.dot(sel, sums[j * 256 : (j + 1) * 256, :], preferred_element_type=jnp.float32)
        packed[j * 16 : (j + 1) * 16, :] = part.astype(jnp.bfloat16)
    out_ref[...] = lax.dot_general(
        slot_ref[...],
        packed[...],
        (((1,), (1,)), ((), ())),
        preferred_element_type=jnp.float32,
    ).astype(jnp.bfloat16)


def gram_sums(by_point, table, row_weights, slots):
    count = table.shape[1] // 2
    halves = (by_point.shape[2] // LANES + 1) // 2
    vmem = pl.BlockSpec(memory_space=pltpu.VMEM)
    return pl.pallas_call(
        gram_body,
        out_shape=jax.ShapeDtypeStruct((slots.shape[0], 256), jnp.bfloat16),
        in_specs=[vmem] * 4,
        out_specs=vmem,
        scratch_shapes=[
            pltpu.VMEM((halves, 256, 2 * count), jnp.bfloat16),
            pltpu.VMEM((halves, 384, 2 * count), jnp.bfloat16),
            pltpu.VMEM((256 * 16, count), jnp.bfloat16),
            pltpu.VMEM((256, count), jnp.bfloat16),
        ],
        compiler_params=pltpu.CompilerParams(vmem_limit_bytes=24 * 1024 * 1024),
        name="gram_sums",
    )(by_point, table, row_weights, slots)


def unpack_matrix(blocks):
    table = np.zeros((256, 2 * blocks * blocks), np.float32)
    half = blocks // 2
    for b in range(blocks):
        for e in range(blocks):
            delta = (e - b) % blocks
            if delta < half:
                real, imag, sign = 16 * delta + b, 16 * (delta + 7) + b, 1.0
            elif delta == half:
                real, imag, sign = 240 + b % half, 248 + b % half, 1.0 if b < half else -1.0
            else:
                back = blocks - delta
                real, imag, sign = 16 * back + e, 16 * (back + 7) + e, -1.0
            table[real, b * blocks + e] = 1.0
            if delta:
                table[imag, blocks * blocks + b * blocks + e] = sign
    return table


def shards(snapshots, weights, freq_bins, bin_owners):
    blocks, local_steps, fields, points = snapshots.shape
    tm_count = lax.axis_size("tm")
    pts_count = lax.axis_size("pts")
    fft_len = local_steps * tm_count
    sub_points = points // tm_count
    slot_count = tm_count * CAP
    sent = scatter_points(jnp.transpose(snapshots, (0, 2, 1, 3)))
    by_point = lax.all_to_all(sent, "tm", split_axis=0, concat_axis=0, tiled=True)
    table = dft_columns(freq_bins, fft_len)
    slots = slot_rows(bin_owners, slot_count)
    mine = lax.dynamic_slice(weights, (0, lax.axis_index("tm") * sub_points), (fields, sub_points))
    paired = jnp.broadcast_to(
        mine[: fields - 1].reshape(fields // 2, 1, 2, sub_points),
        (fields // 2, blocks, 2, sub_points),
    )
    single = jnp.broadcast_to(mine[fields - 1 :], (blocks, sub_points))
    row_weights = jnp.concatenate([paired.reshape(-1), single.reshape(-1)])
    row_weights = jnp.broadcast_to(row_weights[:, None], (row_weights.shape[0], LANES))
    partial = gram_sums(by_point, table, row_weights, slots)
    partial = partial.reshape(tm_count, CAP, 256)
    partial = lax.all_to_all(partial, "tm", split_axis=0, concat_axis=0, tiled=True)
    owned = jnp.sum(partial.astype(jnp.float32), axis=0)
    copies = jnp.broadcast_to(owned[None], (pts_count,) + owned.shape)
    copies = lax.all_to_all(copies, "pts", split_axis=0, concat_axis=0, tiled=True)
    summed = jnp.sum(copies, axis=0)
    return jnp.dot(
        summed, jnp.asarray(unpack_matrix(blocks)), precision=lax.Precision.HIGHEST
    )


def solution(mesh):
    in_specs = (P(None, "tm", None, "pts"), P(None, "pts"), P(), P())
    out_specs = P("tm", None)
    return jax.shard_map(shards, mesh=mesh, in_specs=in_specs, out_specs=out_specs, check_vma=False)
```

time: 96 us -> 76.9 us (0.80)
  blocking collectives: 52.1 us -> 41.3 us
  Pallas kernels: 12.2 us -> 4.8 us
  other arithmetic: 5.7 us -> 2.7 us
  local copies, waits for them, and re-layouts: 1.66 us -> 2.81 us
  waiting for transfers between devices: 12.2 us -> 13.3 us
    pallas_call x1, Pallas kernels: 9.44 us -> 2.09 us  [gram_sums(): pl.pallas_call(gram_body, out_shape=jax.ShapeDtypeStruct((slots.shape[0],...]
    all_to_all x2 -> x1, blocking collectives: 31.3 us -> 25.6 us  [shards(): lax.all_to_all(copies, 'pts', split_axis=0, concat_axis=0, tiled=True)]
    all_to_all x1, blocking collectives: 20.8 us -> 15.7 us  [shards(): lax.all_to_all(partial, 'tm', split_axis=0, concat_axis=0, tiled=True)]
    convert_element_type x2 -> x1, other arithmetic: 3.79 us -> 2.29 us  [dft_columns(): cosine = (scaled * jnp.cos(angles)).astype(jnp.bfloat16)]
    all_to_all x1, waiting for transfers between devices: 12.2 us -> 13.3 us  [shards(): lax.all_to_all(sent, 'tm', split_axis=0, concat_axis=0, tiled=True)]
  transfers between devices with their start and end apart: 1 -> 1, of which waited for: 1 -> 1; matrix products, arithmetic and copies ran while one was open for 7% -> 4% of each run, Pallas kernels for 0% -> 0%
where the time goes in v2:
time: 76.9 us; the launch traced here: 76.6 us
  blocking collectives  41.3 us (54%)
  waiting for transfers between devices  13.3 us (17%)
  starting transfers between devices  10.5 us (14%)
  Pallas kernels  4.8 us (6%)
  local copies, waits for them, and re-layouts  2.81 us (4%)
  other arithmetic  2.7 us (4%)
  matrix products  0.99 us (1%)
    all_to_all x1, blocking collectives, shards(): lax.all_to_all(copies, 'pts', split_axis=0, concat_axis=0, tiled=True)  25.6 us
    all_to_all x1, blocking collectives, shards(): lax.all_to_all(partial, 'tm', split_axis=0, concat_axis=0, tiled=True)  15.7 us
    all_to_all x1, waiting for transfers between devices, shards(): lax.all_to_all(sent, 'tm', split_axis=0, concat_axis=0, tiled=True)  13.3 us
    all_to_all x1, starting transfers between devices, shards(): lax.all_to_all(sent, 'tm', split_axis=0, concat_axis=0, tiled=True)  10.5 us
    pallas_call x1, Pallas kernels, scatter_points(): pl.pallas_call(scatter_body, grid=(tiles,), out_shape=jax.ShapeDtypeStruc...  2.71 us
    convert_element_type x1, other arithmetic, dft_columns(): cosine = (scaled * jnp.cos(angles)).astype(jnp.bfloat16)  2.29 us
    pallas_call x1, Pallas kernels, gram_sums(): pl.pallas_call(gram_body, out_shape=jax.ShapeDtypeStruct((slots.shape[0],...  2.09 us
    unnamed x10, local copies, waits for them, and re-layouts  1.78 us
  transfers between devices with their start and end apart: 1, of which 1 were waited for; matrix products, arithmetic and copies ran while one was open for 4% of the time, Pallas kernels for 0%

profile of v2, /device:TPU:1, one launch (start us, length us, event | category | flops | bytes accessed | tf_op | source)
XLA Modules:
  0.0 76.6 jit_solution(15507741791153760367)
XLA Ops:
  0.0 0.0 copy-start
  0.0 2.7 %scatter_points.1 = bf16[32,16,640]{2,1,0:T(8,128)(2,1)} custom-call(bf16[16,5,16,256]{3,2,1,0:T(8,128)(2,1)} %bitcast.8), custom_call_target="tpu_custom_call" | custom-call | tf_op jit(solution)/shard_map/scatter_points/pallas_call | solution.py:66
  2.7 10.5 %all-to-all-start = ((bf16[32,16,640]{2,1,0:T(8,128)(2,1)}), bf16[32,16,640]{2,1,0:T(8,128)(2,1)S(1)}, u32[]{:S(2)}, u32[]{:S(2)}) async-start(bf16[32,16,640]{2,1,0:T(8,128)(2,1)} %scatter_points.1), calls=%async_computation | async-start | bytes 1310720 | tf_op jit(solution)/shard_map/all_to_all | solution.py:188
  13.2 0.0 copy-done
  13.2 0.1 constant_dynamic-slice_fusion
  13.3 0.0 copy-start.3
  13.3 0.6 copy-done.3
  13.9 0.0 slice-start
  13.9 0.1 reshape.37
  14.0 0.6 slice-done
  14.6 0.0 copy-start.2
  14.6 0.1 reshape.36
  14.8 0.5 copy-done.2
  15.3 0.2 convert_reduce_fusion.1
  15.4 0.0 copy-start.4
  15.5 0.7 copy-done.4
  16.1 2.3 %multiply_convert_fusion.1 = (bf16[512,256]{1,0:T(8,128)(2,1)S(1)}, bf16[512,256]{1,0:T(8,128)(2,1)S(1)}) fusion(s32[256]{0:T(256)S(1)} %copy-done.4, f32[512]{0:T(512)S(1)} %get-tuple-element.7, f32[512]{0:T(512)S(1)} %get-tuple-element.8), kind=kLoop, calls=%fused_computation.10 | loop fusion | flops 2359296 | bytes 529408 | tf_op jit(solution)/shard_map/convert_element_type | solution.py:21
  18.5 0.1 fusion.6.slot_ref
  18.6 13.3 %all-to-all-done.x_ref = bf16[32,16,640]{2,1,0:T(8,128)(2,1)S(1)} async-done(((bf16[32,16,640]{2,1,0:T(8,128)(2,1)}), bf16[32,16,640]{2,1,0:T(8,128)(2,1)S(1)}, u32[]{:S(2)}, u32[]{:S(2)}) %all-to-all-start) | async-done | bytes 655392 | tf_op jit(solution)/shard_map/all_to_all | solution.py:188
  31.9 0.1 broadcast_in_dim.16.w_ref
  32.0 2.1 %gram_sums.1 = bf16[512,256]{1,0:T(8,128)(2,1)S(1)} custom-call(bf16[32,16,640]{2,1,0:T(8,128)(2,1)S(1)} %all-to-all-done.x_ref, bf16[512,512]{1,0:T(8,128)(2,1)S(1)} %pad_maximum_fusion.table_ref, f32[640,128]{1,0:T(8,128)S(1)} %broadcast_in_dim.16.w_ref, bf16[512,256]{1,0:T(8,128)(2,1)S(1)} %fusion.6.slot_ref), custom_call_target="tpu_custom_call" | custom-call | tf_op jit(solution)/shard_map/gram_sums/pallas_call | solution.py:145
  34.1 15.7 %all_to_all.15 = bf16[32,16,256]{2,1,0:T(8,128)(2,1)S(1)} all-to-all(bf16[32,16,256]{2,1,0:T(8,128)(2,1)S(1)} %bitcast.7), channel_id=1, replica_groups=mesh['tm'=32,'pts'=16] {'tm'}, dimensions={0} | all-to-all | bytes 524288 | tf_op jit(solution)/shard_map/all_to_all | solution.py:201
  49.9 0.0 copy-start.1
  49.9 25.6 %all_to_all.16 = f32[16,16,256]{2,1,0:T(8,128)S(1)} all-to-all(f32[16,16,256]{2,1,0:T(8,128)S(1)} %broadcast_in_dim.17), channel_id=1, replica_groups=mesh['tm'=32,'pts'=16] {'pts'}, dimensions={0} | all-to-all | bytes 524288 | tf_op jit(solution)/shard_map/all_to_all | solution.py:204
  75.6 0.0 copy-done.1
  75.6 1.0 %fusion.9 = f32[16,512]{1,0:T(8,128)} fusion(f32[16,256]{1,0:T(8,128)S(1)} %reduce_sum.29, f32[256,512]{1,0:T(8,128)S(1)} %copy-done.1), kind=kOutput, calls=%fused_computation.24 | convolution fusion | flops 25165824 | bytes 573440 | tf_op jit(solution)/shard_map/dot_general | solution.py:206
  (10 shorter events, 0.2 us)
Async XLA Ops:
  0.0 13.2 %copy-start = (f32[5,256]{1,0:T(8,128)S(1)}, f32[5,256]{1,0:T(8,128)}, u32[]{:S(2)}) copy-start(f32[5,256]{1,0:T(8,128)} %param.6) | copy-start | bytes 15364
  2.7 29.2 %all-to-all-start = ((bf16[32,16,640]{2,1,0:T(8,128)(2,1)}), bf16[32,16,640]{2,1,0:T(8,128)(2,1)S(1)}, u32[]{:S(2)}, u32[]{:S(2)}) async-start(bf16[32,16,640]{2,1,0:T(8,128)(2,1)} %scatter_points.1), calls=%async_computation | async-start | bytes 1310720 | tf_op jit(solution)/shard_map/all_to_all | solution.py:188
  13.3 0.6 copy-start.3
  13.9 0.7 slice-start
  14.6 0.7 copy-start.2
  15.4 0.7 copy-start.4
  49.9 25.7 %copy-start.1 = (f32[256,512]{1,0:T(8,128)S(1)}, f32[256,512]{1,0:T(8,128)}, u32[]{:S(2)}) copy-start(f32[256,512]{1,0:T(8,128)} %constant.47.clone) | copy-start | bytes 1572868

commit v3 on v2

v3 whole, which is shorter than its diff:
```python
import functools

import jax
import jax.numpy as jnp
import numpy as np
from jax import lax
from jax.experimental import pallas as pl
from jax.experimental.pallas import tpu as pltpu
from jax.sharding import PartitionSpec as P

CAP = 16
LANES = 128


def dft_columns(bin_values, fft_len):
    steps_t = jnp.arange(fft_len, dtype=jnp.int32)[:, None]
    wound = bin_values[None, :] * steps_t % fft_len
    angles = 2.0 * jnp.pi * wound.astype(jnp.float32) / fft_len
    hann_window = 0.5 - 0.5 * jnp.cos(2.0 * jnp.pi * steps_t.astype(jnp.float32) / fft_len)
    scaled = hann_window / jnp.sqrt(jnp.float32(3.0 * fft_len / 8.0))
    cosine = (scaled * jnp.cos(angles)).astype(jnp.bfloat16)
    sine_rows = (-scaled * jnp.sin(angles)).astype(jnp.bfloat16)
    return jnp.concatenate([cosine, sine_rows], axis=1)


def slot_rows(bin_owners, owner_count, core):
    count = bin_owners.shape[0]
    listed = jnp.arange(count, dtype=jnp.int32)
    same = (bin_owners[:, None] == bin_owners[None, :]) & (listed[None, :] < listed[:, None])
    position = jnp.sum(same.astype(jnp.int32), axis=1)
    part = CAP // 2
    side = position // part
    row = (side != core).astype(jnp.int32) * (owner_count * part)
    row = row + bin_owners * part + position % part
    return (jnp.arange(owner_count * CAP, dtype=jnp.int32)[:, None] == row[None, :]).astype(
        jnp.bfloat16
    )


def lane_tiles(blocks, fields):
    tiles = []
    for pair in range(fields // 2):
        for first in range(0, blocks, 8):
            tiles.append([(first + g // 2, 2 * pair + g % 2) for g in range(16)])
    return tiles + [[(g, fields - 1) for g in range(16)]]


def scatter_body(x_ref, out_ref, held, ready, arrived, left):
    blocks, fields, steps, points = x_ref.shape
    groups = 16
    width = LANES // groups
    group = lax.broadcasted_iota(jnp.int32, (steps, LANES), 1) // width
    tiles = lane_tiles(blocks, fields)
    copies = []
    for tile, source in enumerate(tiles):
        firsts, lasts = source[0], source[-1]
        part = (slice(firsts[0], lasts[0] + 1), slice(firsts[1], lasts[1] + 1))
        copies.append(pltpu.make_async_copy(x_ref.at[part], held.at[part], arrived.at[tile]))
        copies[-1].start()
    for tile, source in enumerate(tiles):
        copies[tile].wait()
        for h in range(points // LANES):
            rows = []
            for g, (b, f) in enumerate(source):
                row = held[b, f, :, h * LANES : (h + 1) * LANES]
                rows.append(pltpu.roll(row, width * g, 1) if g else row)
            bit = 1
            while bit < groups:
                take = (group & bit) != 0
                rows = [jnp.where(take, rows[(c + bit) % groups], rows[c]) for c in range(groups)]
                bit *= 2
            for d in range(groups):
                row = rows[(groups - d) % groups]
                if d:
                    row = pltpu.roll(row, LANES - width * d, 1)
                ready[tile, h * groups + d] = row
        lanes = slice(tile * LANES, (tile + 1) * LANES)
        copies[tile] = pltpu.make_async_copy(ready.at[tile], out_ref.at[:, :, lanes], left.at[tile])
        copies[tile].start()
    for copy in copies:
        copy.wait()


def scatter_points(x):
    blocks, fields, steps, points = x.shape
    tiles = len(lane_tiles(blocks, fields))
    wide = tiles * LANES
    return pl.pallas_call(
        scatter_body,
        out_shape=jax.ShapeDtypeStruct((points // 8, steps, wide), jnp.bfloat16),
        in_specs=[pl.BlockSpec(memory_space=pltpu.HBM)],
        out_specs=pl.BlockSpec(memory_space=pltpu.HBM),
        scratch_shapes=[
            pltpu.VMEM(x.shape, jnp.bfloat16),
            pltpu.VMEM((tiles, points // 8, steps, LANES), jnp.bfloat16),
            pltpu.SemaphoreType.DMA((tiles,)),
            pltpu.SemaphoreType.DMA((tiles,)),
        ],
        name="scatter_points",
    )(x)


def split2(value):
    high = value.astype(jnp.bfloat16)
    return high, (value - high.astype(jnp.float32)).astype(jnp.bfloat16)


def gram_body(x_ref, table_ref, w_ref, slot_ref, keep_ref, send_ref, plain, weighted, sums, high, low):
    steps = x_ref.shape[0] * x_ref.shape[1]
    count = table_ref.shape[1] // 2
    tiles = x_ref.shape[2] // LANES
    for tile in range(tiles):
        cols = slice(tile * LANES, (tile + 1) * LANES)
        spec = lax.dot_general(
            x_ref[:, :, cols].reshape(steps, LANES),
            table_ref[...],
            (((0,), (0,)), ((), ())),
            preferred_element_type=jnp.float32,
        )
        spec = spec.astype(jnp.bfloat16).astype(jnp.float32)
        scaled = spec * jnp.concatenate([w_ref[cols, :]] * (2 * count // LANES), axis=1)
        scaled = scaled.astype(jnp.bfloat16).astype(jnp.float32)
        each = 16 if tile < tiles - 1 else 8
        at = tile // 2 * 16
        some = LANES // each
        first = tile % 2 * some if tile < tiles - 1 else 0
        spec = spec.reshape(some, each, 2 * count)
        scaled = scaled.reshape(some, each, 2 * count)
        plain[first : first + some, at : at + each, :] = spec
        weighted[first : first + some, at : at + each, :] = scaled
        if first == 0:
            weighted[16:24, at : at + each, :] = scaled[:8]
    depth = plain.shape[1]

    def block(b, last):
        for lane in range(0, count, LANES):
            re = plain[b, :, lane : lane + LANES]
            im = plain[b, :, count + lane : count + lane + LANES]
            for delta in range(last + 1):
                qre = weighted[b + delta, :, lane : lane + LANES]
                qim = weighted[b + delta, :, count + lane : count + lane + LANES]
                real = (re * qre + im * qim).reshape(depth // 8, 8, LANES)
                where = delta if delta < 8 else 15
                sums[where * 16 + b, :, lane : lane + LANES] = jnp.sum(real, axis=0)
                if delta:
                    imag = (re * qim - im * qre).reshape(depth // 8, 8, LANES)
                    offset = (delta + 7) * 16 if delta < 8 else 15 * 16 + 8
                    sums[offset + b, :, lane : lane + LANES] = jnp.sum(imag, axis=0)

    lax.fori_loop(0, 8, lambda b, carry: (block(b, 8), carry)[1], 0)
    lax.fori_loop(8, 16, lambda b, carry: (block(b, 7), carry)[1], 0)
    sel = lax.broadcasted_iota(jnp.int32, (32, 256), 1) // 8
    sel = (sel == lax.broadcasted_iota(jnp.int32, (32, 256), 0)).astype(jnp.bfloat16)
    for j in range(8):
        hi, lo = split2(sums[j * 32 : (j + 1) * 32].reshape(256, count))
        part = jnp.dot(sel, hi, preferred_element_type=jnp.float32)
        part += jnp.dot(sel, lo, preferred_element_type=jnp.float32)
        high[j * 32 : (j + 1) * 32, :], low[j * 32 : (j + 1) * 32, :] = split2(part)
    half = keep_ref.shape[0]
    for ref, at in ((send_ref, half), (keep_ref, 0)):
        rows = slot_ref[at : at + half, :]
        dims = (((1,), (1,)), ((), ()))
        ref[...] = lax.dot_general(
            rows, high[...], dims, preferred_element_type=jnp.float32
        ) + lax.dot_general(rows, low[...], dims, preferred_element_type=jnp.float32)


def gram_sums(by_point, table, row_weights, slots):
    count = table.shape[1] // 2
    depth = by_point.shape[2] // 16
    vmem = pl.BlockSpec(memory_space=pltpu.VMEM)
    half = jax.ShapeDtypeStruct((slots.shape[0] // 2, 256), jnp.float32)
    return pl.pallas_call(
        gram_body,
        out_shape=(half, half),
        in_specs=[vmem] * 4,
        out_specs=(vmem, vmem),
        scratch_shapes=[
            pltpu.VMEM((16, depth, 2 * count), jnp.float32),
            pltpu.VMEM((24, depth, 2 * count), jnp.float32),
            pltpu.VMEM((256, 8, count), jnp.float32),
            pltpu.VMEM((256, count), jnp.bfloat16),
            pltpu.VMEM((256, count), jnp.bfloat16),
        ],
        compiler_params=pltpu.CompilerParams(vmem_limit_bytes=24 * 1024 * 1024),
        name="gram_sums",
    )(by_point, table, row_weights, slots)


def unpack_matrix(blocks):
    table = np.zeros((256, 2 * blocks * blocks), np.float32)
    half = blocks // 2
    for b in range(blocks):
        for e in range(blocks):
            delta = (e - b) % blocks
            if delta < half:
                real, imag, sign = 16 * delta + b, 16 * (delta + 7) + b, 1.0
            elif delta == half:
                real, imag, sign = 240 + b % half, 248 + b % half, 1.0 if b < half else -1.0
            else:
                back = blocks - delta
                real, imag, sign = 16 * back + e, 16 * (back + 7) + e, -1.0
            table[real, b * blocks + e] = 1.0
            if delta:
                table[imag, blocks * blocks + b * blocks + e] = sign
    return table


def shards(snapshots, weights, freq_bins, bin_owners):
    blocks, local_steps, fields, points = snapshots.shape
    tm_count = lax.axis_size("tm")
    pts_count = lax.axis_size("pts")
    fft_len = local_steps * tm_count
    sub_points = points // tm_count
    sent = scatter_points(jnp.transpose(snapshots, (0, 2, 1, 3)))
    by_point = lax.all_to_all(sent, "tm", split_axis=0, concat_axis=0, tiled=True)
    table = dft_columns(freq_bins, fft_len)
    slots = slot_rows(bin_owners, tm_count, lax.axis_index("pts") & 1)
    mine = lax.dynamic_slice(weights, (0, lax.axis_index("tm") * sub_points), (fields, sub_points))
    paired = jnp.broadcast_to(
        mine[: fields - 1].reshape(fields // 2, 1, 2, sub_points),
        (fields // 2, blocks, 2, sub_points),
    )
    single = jnp.broadcast_to(mine[fields - 1 :], (blocks, sub_points))
    row_weights = jnp.concatenate([paired.reshape(-1), single.reshape(-1)])
    row_weights = jnp.broadcast_to(row_weights[:, None], (row_weights.shape[0], LANES))
    keep, send = gram_sums(by_point, table, row_weights, slots)
    pairs = [(i, i ^ 1) for i in range(pts_count)]
    partial = (keep + lax.ppermute(send, "pts", pairs)).reshape(tm_count, CAP // 2, 256)
    partial = lax.all_to_all(partial, "tm", split_axis=0, concat_axis=0, tiled=True)
    owned = jnp.sum(partial, axis=0)
    copies = jnp.broadcast_to(owned[None], (pts_count,) + owned.shape)
    copies = lax.all_to_all(copies, "pts", split_axis=0, concat_axis=0, tiled=True)
    summed = jnp.sum(copies.reshape(pts_count // 2, CAP, 256), axis=0)
    return jnp.dot(
        summed, jnp.asarray(unpack_matrix(blocks)), precision=lax.Precision.HIGHEST
    )


def solution(mesh):
    in_specs = (P(None, "tm", None, "pts"), P(None, "pts"), P(), P())
    out_specs = P("tm", None)
    return jax.shard_map(shards, mesh=mesh, in_specs=in_specs, out_specs=out_specs, check_vma=False)
```

time: 76.9 us -> 79.4 us (1.033)
  starting transfers between devices: 10.5 us -> 14.9 us
  blocking collectives: 41.3 us -> 37.5 us
  waiting for transfers between devices: 13.3 us -> 14.5 us
    ppermute x0 -> x1, starting transfers between devices: none -> 4.39 us  [shards(): lax.ppermute(send, 'pts', pairs)]
    all_to_all x1, blocking collectives: 25.6 us -> 21.4 us  [shards(): lax.all_to_all(copies, 'pts', split_axis=0, concat_axis=0, tiled=True)]
    ppermute x0 -> x1, waiting for transfers between devices: none -> 1.14 us  [shards(): lax.ppermute(send, 'pts', pairs)]
  transfers between devices with their start and end apart: 1 -> 2, of which waited for: 1 -> 2; matrix products, arithmetic and copies ran while one was open for 4% -> 4% of each run, Pallas kernels for 0% -> 0%
where the time goes in v3:
time: 79.4 us; the launch traced here: 79 us
  blocking collectives  37.5 us (47%)
  starting transfers between devices  14.9 us (19%)
  waiting for transfers between devices  14.5 us (18%)
  Pallas kernels  5.45 us (7%)
  local copies, waits for them, and re-layouts  2.8 us (4%)
  other arithmetic  2.72 us (3%)
  matrix products  0.99 us (1%)
    all_to_all x1, blocking collectives, shards(): lax.all_to_all(copies, 'pts', split_axis=0, concat_axis=0, tiled=True)  21.4 us
    all_to_all x1, blocking collectives, shards(): lax.all_to_all(partial, 'tm', split_axis=0, concat_axis=0, tiled=True)  16.1 us
    all_to_all x1, waiting for transfers between devices, shards(): lax.all_to_all(sent, 'tm', split_axis=0, concat_axis=0, tiled=True)  13.3 us
    all_to_all x1, starting transfers between devices, shards(): lax.all_to_all(sent, 'tm', split_axis=0, concat_axis=0, tiled=True)  10.5 us
    ppermute x1, starting transfers between devices, shards(): lax.ppermute(send, 'pts', pairs)  4.39 us
    pallas_call x1, Pallas kernels, gram_sums(): pl.pallas_call(gram_body, out_shape=(half, half), in_specs=[vmem] * 4, ou...  2.78 us
    pallas_call x1, Pallas kernels, scatter_points(): pl.pallas_call(scatter_body, out_shape=jax.ShapeDtypeStruct((points // 8,...  2.67 us
    convert_element_type x1, other arithmetic, dft_columns(): cosine = (scaled * jnp.cos(angles)).astype(jnp.bfloat16)  2.29 us
  transfers between devices with their start and end apart: 2, of which 2 were waited for; matrix products, arithmetic and copies ran while one was open for 4% of the time, Pallas kernels for 0%

profile of v3, /device:TPU:1, one launch (start us, length us, event | category | flops | bytes accessed | tf_op | source)
XLA Modules:
  0.0 79.0 jit_solution(15217019685512333895)
XLA Ops:
  0.0 0.0 copy-start
  0.0 2.7 %scatter_points.1 = bf16[32,16,640]{2,1,0:T(8,128)(2,1)} custom-call(bf16[16,5,16,256]{3,2,1,0:T(8,128)(2,1)} %bitcast.11), custom_call_target="tpu_custom_call" | custom-call | tf_op jit(solution)/shard_map/scatter_points/pallas_call | solution.py:88
  2.7 10.5 %all-to-all-start = ((bf16[32,16,640]{2,1,0:T(8,128)(2,1)}), bf16[32,16,640]{2,1,0:T(8,128)(2,1)S(1)}, u32[]{:S(2)}, u32[]{:S(2)}) async-start(bf16[32,16,640]{2,1,0:T(8,128)(2,1)} %scatter_points.1), calls=%async_computation | async-start | bytes 1310720 | tf_op jit(solution)/shard_map/all_to_all | solution.py:216
  13.2 0.0 copy-done
  13.2 0.1 constant_dynamic-slice_fusion
  13.3 0.0 copy-start.3
  13.3 0.6 copy-done.3
  13.9 0.0 slice-start
  13.9 0.1 reshape.40
  14.0 0.6 slice-done
  14.6 0.0 copy-start.2
  14.6 0.1 reshape.39
  14.8 0.5 copy-done.2
  15.3 0.2 convert_reduce_fusion
  15.4 0.0 copy-start.4
  15.4 0.7 copy-done.4
  16.1 2.3 %multiply_convert_fusion.1 = (bf16[512,256]{1,0:T(8,128)(2,1)S(1)}, bf16[512,256]{1,0:T(8,128)(2,1)S(1)}) fusion(s32[256]{0:T(256)S(1)} %copy-done.4, f32[512]{0:T(512)S(1)} %get-tuple-element.11, f32[512]{0:T(512)S(1)} %get-tuple-element.12), kind=kLoop, calls=%fused_computation.9 | loop fusion | flops 2359296 | bytes 529408 | tf_op jit(solution)/shard_map/convert_element_type | solution.py:21
  18.5 0.1 fusion.6.slot_ref
  18.6 13.3 %all-to-all-done.x_ref = bf16[32,16,640]{2,1,0:T(8,128)(2,1)S(1)} async-done(((bf16[32,16,640]{2,1,0:T(8,128)(2,1)}), bf16[32,16,640]{2,1,0:T(8,128)(2,1)S(1)}, u32[]{:S(2)}, u32[]{:S(2)}) %all-to-all-start) | async-done | bytes 655392 | tf_op jit(solution)/shard_map/all_to_all | solution.py:216
  31.9 0.1 broadcast_in_dim.16.w_ref
  32.0 2.8 %gram_sums.1 = (f32[256,256]{1,0:T(8,128)S(1)}, f32[256,256]{1,0:T(8,128)S(1)}) custom-call(bf16[32,16,640]{2,1,0:T(8,128)(2,1)S(1)} %all-to-all-done.x_ref, bf16[512,512]{1,0:T(8,128)(2,1)S(1)} %pad_maximum_fusion.table_ref, f32[640,128]{1,0:T(8,128)S(1)} %broadcast_in_dim.16.w_ref, bf16[512,256]{1,0:T(8,128)(2,1)S(1)} %fusion.6.slot_ref), custom_call_target="tpu_custom_call" | custom-call | tf_op jit(solution)/shard_map/gram_sums/pallas_call | solution.py:173
  34.8 4.4 %collective-permute-start = (f32[256,256]{1,0:T(8,128)S(1)}, f32[256,256]{1,0:T(8,128)S(1)}, u32[]{:S(2)}, u32[]{:S(2)}) collective-permute-start(f32[256,256]{1,0:T(8,128)S(1)} %get-tuple-element.8), channel_id=1, source_target_pairs={{0,1},{1,0},{2,3},{3,2},{4,5},{5,4},{6,7},{7,6},{8,9},{9,8},{10,11... | collective-permute-start | bytes 786440 | tf_op jit(solution)/shard_map/ppermute | solution.py:229
  39.2 1.1 %collective-permute-done = f32[256,256]{1,0:T(8,128)S(1)} collective-permute-done((f32[256,256]{1,0:T(8,128)S(1)}, f32[256,256]{1,0:T(8,128)S(1)}, u32[]{:S(2)}, u32[]{:S(2)}) %collective-permute-start) | collective-permute-done | bytes 262176 | tf_op jit(solution)/shard_map/ppermute | solution.py:229
  40.4 16.1 %all_to_all.15 = f32[32,8,256]{2,1,0:T(8,128)S(1)} all-to-all(f32[32,8,256]{2,1,0:T(8,128)S(1)} %add_bitcast_fusion), channel_id=1, replica_groups=mesh['tm'=32,'pts'=16] {'tm'}, dimensions={0} | all-to-all | bytes 524288 | tf_op jit(solution)/shard_map/all_to_all | solution.py:230
  56.5 0.0 copy-start.1
  56.5 21.4 %all_to_all.16 = f32[16,8,256]{2,1,0:T(8,128)S(1)} all-to-all(f32[16,8,256]{2,1,0:T(8,128)S(1)} %broadcast_in_dim.17), channel_id=1, replica_groups=mesh['tm'=32,'pts'=16] {'pts'}, dimensions={0} | all-to-all | bytes 262144 | tf_op jit(solution)/shard_map/all_to_all | solution.py:233
  78.0 0.0 copy-done.1
  78.0 1.0 %fusion.11 = f32[16,512]{1,0:T(8,128)} fusion(f32[16,256]{1,0:T(8,128)S(1)} %bitcast_reduce_fusion, f32[256,512]{1,0:T(8,128)S(1)} %copy-done.1), kind=kOutput, calls=%fused_computation.32 | convolution fusion | flops 25165824 | bytes 573440 | tf_op jit(solution)/shard_map/dot_general | solution.py:235
  (11 shorter events, 0.2 us)
Async XLA Ops:
  0.0 13.2 %copy-start = (f32[5,256]{1,0:T(8,128)S(1)}, f32[5,256]{1,0:T(8,128)}, u32[]{:S(2)}) copy-start(f32[5,256]{1,0:T(8,128)} %param.6) | copy-start | bytes 15364
  2.7 29.2 %all-to-all-start = ((bf16[32,16,640]{2,1,0:T(8,128)(2,1)}), bf16[32,16,640]{2,1,0:T(8,128)(2,1)S(1)}, u32[]{:S(2)}, u32[]{:S(2)}) async-start(bf16[32,16,640]{2,1,0:T(8,128)(2,1)} %scatter_points.1), calls=%async_computation | async-start | bytes 1310720 | tf_op jit(solution)/shard_map/all_to_all | solution.py:216
  13.3 0.6 copy-start.3
  13.9 0.7 slice-start
  14.6 0.7 copy-start.2
  15.4 0.7 copy-start.4
  34.8 5.5 %collective-permute-start = (f32[256,256]{1,0:T(8,128)S(1)}, f32[256,256]{1,0:T(8,128)S(1)}, u32[]{:S(2)}, u32[]{:S(2)}) collective-permute-start(f32[256,256]{1,0:T(8,128)S(1)} %get-tuple-element.8), channel_id=1, source_target_pairs={{0,1},{1,0},{2,3},{3,2},{4,5},{5,4},{6,7},{7,6},{8,9},{9,8},{10,11... | collective-permute-start | bytes 786440 | tf_op jit(solution)/shard_map/ppermute | solution.py:229
  56.5 21.5 %copy-start.1 = (f32[256,512]{1,0:T(8,128)S(1)}, f32[256,512]{1,0:T(8,128)}, u32[]{:S(2)}) copy-start(f32[256,512]{1,0:T(8,128)} %constant.77.clone) | copy-start | bytes 1572868

commit v4 on v3

--- a/solution.py
+++ b/solution.py
@@ -10,10 +10,21 @@
 
 CAP = 16
 LANES = 128
-
-
-def dft_columns(bin_values, fft_len):
-    steps_t = jnp.arange(fft_len, dtype=jnp.int32)[:, None]
+FIRST_POINTS = 18
+FIRST_SLOTS = 18
+FIRST_SUMS = 14
+
+
+def exchange(value, axis, first):
+    size = lax.axis_size(axis)
+    order = [[(c + first) % size for c in range(size)]]
+    return lax.all_to_all(
+        value, axis, split_axis=0, concat_axis=0, tiled=True, axis_index_groups=order
+    )
+
+
+def dft_columns(bin_values, fft_len, first_step):
+    steps_t = (jnp.arange(fft_len, dtype=jnp.int32)[:, None] + first_step) % fft_len
     wound = bin_values[None, :] * steps_t % fft_len
     angles = 2.0 * jnp.pi * wound.astype(jnp.float32) / fft_len
     hann_window = 0.5 - 0.5 * jnp.cos(2.0 * jnp.pi * steps_t.astype(jnp.float32) / fft_len)
@@ -31,7 +42,8 @@
     part = CAP // 2
     side = position // part
     row = (side != core).astype(jnp.int32) * (owner_count * part)
-    row = row + bin_owners * part + position % part
+    place = (bin_owners + owner_count - FIRST_SLOTS) % owner_count
+    row = row + place * part + position % part
     return (jnp.arange(owner_count * CAP, dtype=jnp.int32)[:, None] == row[None, :]).astype(
         jnp.bfloat16
     )
@@ -73,7 +85,7 @@
                 row = rows[(groups - d) % groups]
                 if d:
                     row = pltpu.roll(row, LANES - width * d, 1)
-                ready[tile, h * groups + d] = row
+                ready[tile, (h * groups + d - FIRST_POINTS) % (points // 8)] = row
         lanes = slice(tile * LANES, (tile + 1) * LANES)
         copies[tile] = pltpu.make_async_copy(ready.at[tile], out_ref.at[:, :, lanes], left.at[tile])
         copies[tile].start()
@@ -213,8 +225,8 @@
     fft_len = local_steps * tm_count
     sub_points = points // tm_count
     sent = scatter_points(jnp.transpose(snapshots, (0, 2, 1, 3)))
-    by_point = lax.all_to_all(sent, "tm", split_axis=0, concat_axis=0, tiled=True)
-    table = dft_columns(freq_bins, fft_len)
+    by_point = exchange(sent, "tm", FIRST_POINTS)
+    table = dft_columns(freq_bins, fft_len, FIRST_POINTS * local_steps)
     slots = slot_rows(bin_owners, tm_count, lax.axis_index("pts") & 1)
     mine = lax.dynamic_slice(weights, (0, lax.axis_index("tm") * sub_points), (fields, sub_points))
     paired = jnp.broadcast_to(
@@ -227,10 +239,10 @@
     keep, send = gram_sums(by_point, table, row_weights, slots)
     pairs = [(i, i ^ 1) for i in range(pts_count)]
     partial = (keep + lax.ppermute(send, "pts", pairs)).reshape(tm_count, CAP // 2, 256)
-    partial = lax.all_to_all(partial, "tm", split_axis=0, concat_axis=0, tiled=True)
+    partial = exchange(partial, "tm", FIRST_SLOTS)
     owned = jnp.sum(partial, axis=0)
     copies = jnp.broadcast_to(owned[None], (pts_count,) + owned.shape)
-    copies = lax.all_to_all(copies, "pts", split_axis=0, concat_axis=0, tiled=True)
+    copies = exchange(copies, "pts", FIRST_SUMS)
     summed = jnp.sum(copies.reshape(pts_count // 2, CAP, 256), axis=0)
     return jnp.dot(
         summed, jnp.asarray(unpack_matrix(blocks)), precision=lax.Precision.HIGHEST

time: 79.4 us -> 73.2 us (0.922)
  waiting for transfers between devices: 14.5 us -> 7.17 us
  starting transfers between devices: 14.9 us -> 18.6 us
  blocking collectives: 37.5 us -> 34.7 us
    all_to_all x1, waiting for transfers between devices: 13.3 us -> 6.03 us  [exchange(): lax.all_to_all(value, axis, split_axis=0, concat_axis=0, tiled=True, axis...]
    all_to_all x2, blocking collectives: 37.5 us -> 34.7 us  [exchange(): lax.all_to_all(value, axis, split_axis=0, concat_axis=0, tiled=True, axis...]
    all_to_all x1, starting transfers between devices: 10.5 us -> 12.5 us  [exchange(): lax.all_to_all(value, axis, split_axis=0, concat_axis=0, tiled=True, axis...]
    ppermute x1, starting transfers between devices: 4.39 us -> 6.14 us  [shards(): lax.ppermute(send, 'pts', pairs)]
where the time goes in v4:
time: 73.2 us; the launch traced here: 72.8 us
  blocking collectives  34.7 us (47%)
  starting transfers between devices  18.6 us (25%)
  waiting for transfers between devices  7.17 us (10%)
  Pallas kernels  5.45 us (7%)
  other arithmetic  2.95 us (4%)
  local copies, waits for them, and re-layouts  2.79 us (4%)
  matrix products  0.99 us (1%)
    all_to_all x2, blocking collectives, exchange(): lax.all_to_all(value, axis, split_axis=0, concat_axis=0, tiled=True, axis...  34.7 us
    all_to_all x1, starting transfers between devices, exchange(): lax.all_to_all(value, axis, split_axis=0, concat_axis=0, tiled=True, axis...  12.5 us
    ppermute x1, starting transfers between devices, shards(): lax.ppermute(send, 'pts', pairs)  6.14 us
    all_to_all x1, waiting for transfers between devices, exchange(): lax.all_to_all(value, axis, split_axis=0, concat_axis=0, tiled=True, axis...  6.03 us
    pallas_call x1, Pallas kernels, gram_sums(): pl.pallas_call(gram_body, out_shape=(half, half), in_specs=[vmem] * 4, ou...  2.78 us
    pallas_call x1, Pallas kernels, scatter_points(): pl.pallas_call(scatter_body, out_shape=jax.ShapeDtypeStruct((points // 8,...  2.67 us
    convert_element_type x1, other arithmetic, dft_columns(): cosine = (scaled * jnp.cos(angles)).astype(jnp.bfloat16)  2.51 us
    unnamed x10, local copies, waits for them, and re-layouts  1.77 us
  transfers between devices with their start and end apart: 2, of which 2 were waited for; matrix products, arithmetic and copies ran while one was open for 4% of the time, Pallas kernels for 0%

profile of v4, /device:TPU:1, one launch (start us, length us, event | category | flops | bytes accessed | tf_op | source)
XLA Modules:
  0.0 72.8 jit_solution(4925177855278170620)
XLA Ops:
  0.0 0.0 copy-start
  0.0 2.7 %scatter_points.1 = bf16[32,16,640]{2,1,0:T(8,128)(2,1)} custom-call(bf16[16,5,16,256]{3,2,1,0:T(8,128)(2,1)} %bitcast.11), custom_call_target="tpu_custom_call" | custom-call | tf_op jit(solution)/shard_map/scatter_points/pallas_call | solution.py:100
  2.7 12.5 %all-to-all-start = ((bf16[32,16,640]{2,1,0:T(8,128)(2,1)}), bf16[32,16,640]{2,1,0:T(8,128)(2,1)S(1)}, u32[]{:S(2)}, u32[]{:S(2)}) async-start(bf16[32,16,640]{2,1,0:T(8,128)(2,1)} %scatter_points.1), calls=%async_computation | async-start | bytes 1310720 | tf_op jit(solution)/shard_map/all_to_all | solution.py:21
  15.2 0.0 copy-done
  15.2 0.1 constant_dynamic-slice_fusion
  15.3 0.0 copy-start.3
  15.3 0.6 copy-done.3
  15.9 0.0 slice-start
  15.9 0.1 reshape.60
  15.9 0.6 slice-done
  16.5 0.0 copy-start.2
  16.6 0.1 reshape.59
  16.7 0.5 copy-done.2
  17.2 0.2 convert_reduce_fusion
  17.4 0.0 copy-start.4
  17.4 0.7 copy-done.4
  18.1 2.5 %multiply_convert_fusion.1 = (bf16[512,256]{1,0:T(8,128)(2,1)S(1)}, bf16[512,256]{1,0:T(8,128)(2,1)S(1)}) fusion(s32[512]{0:T(512)S(1)} %add_select_fusion.1, s32[256]{0:T(256)S(1)} %copy-done.4, f32[512]{0:T(512)S(1)} %get-tuple-element.11, f32[512]{0:T(512)S(1)} %get-tuple-element.12), kind=kLoop, calls=%fused_computation.11 | loop fusion | flops 2359296 | bytes 531456 | tf_op jit(solution)/shard_map/convert_element_type | solution.py:32
  20.7 0.1 fusion.3.slot_ref
  20.8 6.0 %all-to-all-done.x_ref = bf16[32,16,640]{2,1,0:T(8,128)(2,1)S(1)} async-done(((bf16[32,16,640]{2,1,0:T(8,128)(2,1)}), bf16[32,16,640]{2,1,0:T(8,128)(2,1)S(1)}, u32[]{:S(2)}, u32[]{:S(2)}) %all-to-all-start) | async-done | bytes 655392 | tf_op jit(solution)/shard_map/all_to_all | solution.py:21
  26.8 0.1 broadcast_in_dim.16.w_ref
  26.9 2.8 %gram_sums.1 = (f32[256,256]{1,0:T(8,128)S(1)}, f32[256,256]{1,0:T(8,128)S(1)}) custom-call(bf16[32,16,640]{2,1,0:T(8,128)(2,1)S(1)} %all-to-all-done.x_ref, bf16[512,512]{1,0:T(8,128)(2,1)S(1)} %pad_maximum_fusion.table_ref, f32[640,128]{1,0:T(8,128)S(1)} %broadcast_in_dim.16.w_ref, bf16[512,256]{1,0:T(8,128)(2,1)S(1)} %fusion.3.slot_ref), custom_call_target="tpu_custom_call" | custom-call | tf_op jit(solution)/shard_map/gram_sums/pallas_call | solution.py:185
  29.7 6.1 %collective-permute-start = (f32[256,256]{1,0:T(8,128)S(1)}, f32[256,256]{1,0:T(8,128)S(1)}, u32[]{:S(2)}, u32[]{:S(2)}) collective-permute-start(f32[256,256]{1,0:T(8,128)S(1)} %get-tuple-element.8), channel_id=1, source_target_pairs={{0,1},{1,0},{2,3},{3,2},{4,5},{5,4},{6,7},{7,6},{8,9},{9,8},{10,11... | collective-permute-start | bytes 786440 | tf_op jit(solution)/shard_map/ppermute | solution.py:241
  35.9 1.1 %collective-permute-done = f32[256,256]{1,0:T(8,128)S(1)} collective-permute-done((f32[256,256]{1,0:T(8,128)S(1)}, f32[256,256]{1,0:T(8,128)S(1)}, u32[]{:S(2)}, u32[]{:S(2)}) %collective-permute-start) | collective-permute-done | bytes 262176 | tf_op jit(solution)/shard_map/ppermute | solution.py:241
  37.0 15.9 %all_to_all.15 = f32[32,8,256]{2,1,0:T(8,128)S(1)} all-to-all(f32[32,8,256]{2,1,0:T(8,128)S(1)} %add_bitcast_fusion), channel_id=1, replica_groups={{288,304,320,336,352,368,384,400,416,432,448,464,480,496,0,16,32,48,64,..., dimensions={0} | all-to-all | bytes 524288 | tf_op jit(solution)/shard_map/all_to_all | solution.py:21
  52.9 0.0 copy-start.1
  53.0 18.8 %all_to_all.16 = f32[16,8,256]{2,1,0:T(8,128)S(1)} all-to-all(f32[16,8,256]{2,1,0:T(8,128)S(1)} %broadcast_in_dim.17), channel_id=1, replica_groups={{14,15,0,1,2,3,4,5,6,7,8,9,10,11,12,13},{30,31,16,17,18,19,20,21,22,23,..., dimensions={0} | all-to-all | bytes 262144 | tf_op jit(solution)/shard_map/all_to_all | solution.py:21
  71.8 0.0 copy-done.1
  71.8 1.0 %fusion.11 = f32[16,512]{1,0:T(8,128)} fusion(f32[16,256]{1,0:T(8,128)S(1)} %bitcast_reduce_fusion, f32[256,512]{1,0:T(8,128)S(1)} %copy-done.1), kind=kOutput, calls=%fused_computation.40 | convolution fusion | flops 25165824 | bytes 573440 | tf_op jit(solution)/shard_map/dot_general | solution.py:247
  (12 shorter events, 0.2 us)
Async XLA Ops:
  0.0 15.2 %copy-start = (f32[5,256]{1,0:T(8,128)S(1)}, f32[5,256]{1,0:T(8,128)}, u32[]{:S(2)}) copy-start(f32[5,256]{1,0:T(8,128)} %param.6) | copy-start | bytes 15364
  2.7 24.1 %all-to-all-start = ((bf16[32,16,640]{2,1,0:T(8,128)(2,1)}), bf16[32,16,640]{2,1,0:T(8,128)(2,1)S(1)}, u32[]{:S(2)}, u32[]{:S(2)}) async-start(bf16[32,16,640]{2,1,0:T(8,128)(2,1)} %scatter_points.1), calls=%async_computation | async-start | bytes 1310720 | tf_op jit(solution)/shard_map/all_to_all | solution.py:21
  15.3 0.6 copy-start.3
  15.9 0.7 slice-start
  16.5 0.7 copy-start.2
  17.4 0.7 copy-start.4
  29.7 7.3 %collective-permute-start = (f32[256,256]{1,0:T(8,128)S(1)}, f32[256,256]{1,0:T(8,128)S(1)}, u32[]{:S(2)}, u32[]{:S(2)}) collective-permute-start(f32[256,256]{1,0:T(8,128)S(1)} %get-tuple-element.8), channel_id=1, source_target_pairs={{0,1},{1,0},{2,3},{3,2},{4,5},{5,4},{6,7},{7,6},{8,9},{9,8},{10,11... | collective-permute-start | bytes 786440 | tf_op jit(solution)/shard_map/ppermute | solution.py:241
  52.9 18.9 %copy-start.1 = (f32[256,512]{1,0:T(8,128)S(1)}, f32[256,512]{1,0:T(8,128)}, u32[]{:S(2)}) copy-start(f32[256,512]{1,0:T(8,128)} %constant.103.clone) | copy-start | bytes 1572868

commit v5 on v4

--- a/solution.py
+++ b/solution.py
@@ -12,7 +12,7 @@
 LANES = 128
 FIRST_POINTS = 18
 FIRST_SLOTS = 18
-FIRST_SUMS = 14
+FIRST_SUMS = 12
 
 
 def exchange(value, axis, first):
@@ -82,10 +82,9 @@
                 rows = [jnp.where(take, rows[(c + bit) % groups], rows[c]) for c in range(groups)]
                 bit *= 2
             for d in range(groups):
-                row = rows[(groups - d) % groups]
-                if d:
-                    row = pltpu.roll(row, LANES - width * d, 1)
-                ready[tile, (h * groups + d - FIRST_POINTS) % (points // 8)] = row
+                ready[tile, (h * groups + d - FIRST_POINTS) % (points // 8)] = rows[
+                    (groups - d) % groups
+                ]
         lanes = slice(tile * LANES, (tile + 1) * LANES)
         copies[tile] = pltpu.make_async_copy(ready.at[tile], out_ref.at[:, :, lanes], left.at[tile])
         copies[tile].start()
@@ -121,6 +120,7 @@
     steps = x_ref.shape[0] * x_ref.shape[1]
     count = table_ref.shape[1] // 2
     tiles = x_ref.shape[2] // LANES
+    turn = lax.axis_index("tm") % 16
     for tile in range(tiles):
         cols = slice(tile * LANES, (tile + 1) * LANES)
         spec = lax.dot_general(
@@ -130,18 +130,17 @@
             preferred_element_type=jnp.float32,
         )
         spec = spec.astype(jnp.bfloat16).astype(jnp.float32)
-        scaled = spec * jnp.concatenate([w_ref[cols, :]] * (2 * count // LANES), axis=1)
-        scaled = scaled.astype(jnp.bfloat16).astype(jnp.float32)
-        each = 16 if tile < tiles - 1 else 8
-        at = tile // 2 * 16
-        some = LANES // each
-        first = tile % 2 * some if tile < tiles - 1 else 0
-        spec = spec.reshape(some, each, 2 * count)
-        scaled = scaled.reshape(some, each, 2 * count)
-        plain[first : first + some, at : at + each, :] = spec
-        weighted[first : first + some, at : at + each, :] = scaled
-        if first == 0:
-            weighted[16:24, at : at + each, :] = scaled[:8]
+        for g in range(16):
+            source = (g - turn + 16) % 16
+            if tile < tiles - 1:
+                b, f = tile % 2 * 8 + source // 2, tile // 2 * 2 + source % 2
+            else:
+                b, f = source, tiles - 1
+            at = pl.ds(pl.multiple_of(f * 8, 8), 8)
+            piece = spec[g * 8 : (g + 1) * 8, :]
+            scaled = piece * jnp.concatenate([w_ref[at, :]] * (2 * count // LANES), axis=1)
+            plain[b, at, :] = piece
+            weighted[b, at, :] = scaled.astype(jnp.bfloat16).astype(jnp.float32)
     depth = plain.shape[1]
 
     def block(b, last):
@@ -149,8 +148,9 @@
             re = plain[b, :, lane : lane + LANES]
             im = plain[b, :, count + lane : count + lane + LANES]
             for delta in range(last + 1):
-                qre = weighted[b + delta, :, lane : lane + LANES]
-                qim = weighted[b + delta, :, count + lane : count + lane + LANES]
+                e = (b + delta) % 16
+                qre = weighted[e, :, lane : lane + LANES]
+                qim = weighted[e, :, count + lane : count + lane + LANES]
                 real = (re * qre + im * qim).reshape(depth // 8, 8, LANES)
                 where = delta if delta < 8 else 15
                 sums[where * 16 + b, :, lane : lane + LANES] = jnp.sum(real, axis=0)
@@ -189,7 +189,7 @@
         out_specs=(vmem, vmem),
         scratch_shapes=[
             pltpu.VMEM((16, depth, 2 * count), jnp.float32),
-            pltpu.VMEM((24, depth, 2 * count), jnp.float32),
+            pltpu.VMEM((16, depth, 2 * count), jnp.float32),
             pltpu.VMEM((256, 8, count), jnp.float32),
             pltpu.VMEM((256, count), jnp.bfloat16),
             pltpu.VMEM((256, count), jnp.bfloat16),
@@ -229,13 +229,8 @@
     table = dft_columns(freq_bins, fft_len, FIRST_POINTS * local_steps)
     slots = slot_rows(bin_owners, tm_count, lax.axis_index("pts") & 1)
     mine = lax.dynamic_slice(weights, (0, lax.axis_index("tm") * sub_points), (fields, sub_points))
-    paired = jnp.broadcast_to(
-        mine[: fields - 1].reshape(fields // 2, 1, 2, sub_points),
-        (fields // 2, blocks, 2, sub_points),
-    )
-    single = jnp.broadcast_to(mine[fields - 1 :], (blocks, sub_points))
-    row_weights = jnp.concatenate([paired.reshape(-1), single.reshape(-1)])
-    row_weights = jnp.broadcast_to(row_weights[:, None], (row_weights.shape[0], LANES))
+    row_weights = jnp.broadcast_to(mine[:, :, None], (fields, sub_points, LANES))
+    row_weights = row_weights.reshape(fields * sub_points, LANES)
     keep, send = gram_sums(by_point, table, row_weights, slots)
     pairs = [(i, i ^ 1) for i in range(pts_count)]
     partial = (keep + lax.ppermute(send, "pts", pairs)).reshape(tm_count, CAP // 2, 256)

time: 73.2 us -> 72.1 us (0.985)
  local copies, waits for them, and re-layouts: 2.79 us -> 1.38 us
  waiting for transfers between devices: 7.17 us -> 8.54 us
    all_to_all x1, waiting for transfers between devices: 6.03 us -> 7.4 us  [exchange(): lax.all_to_all(value, axis, split_axis=0, concat_axis=0, tiled=True, axis...]
    unnamed x10 -> x8, local copies, waits for them, and re-layouts: 1.77 us -> 1.14 us
where the time goes in v5:
time: 72.1 us; the launch traced here: 71.8 us
  blocking collectives  34 us (47%)
  starting transfers between devices  18.6 us (26%)
  waiting for transfers between devices  8.54 us (12%)
  Pallas kernels  5.19 us (7%)
  other arithmetic  2.94 us (4%)
  local copies, waits for them, and re-layouts  1.38 us (2%)
  matrix products  0.99 us (1%)
    all_to_all x2, blocking collectives, exchange(): lax.all_to_all(value, axis, split_axis=0, concat_axis=0, tiled=True, axis...  34 us
    all_to_all x1, starting transfers between devices, exchange(): lax.all_to_all(value, axis, split_axis=0, concat_axis=0, tiled=True, axis...  12.5 us
    all_to_all x1, waiting for transfers between devices, exchange(): lax.all_to_all(value, axis, split_axis=0, concat_axis=0, tiled=True, axis...  7.4 us
    ppermute x1, starting transfers between devices, shards(): lax.ppermute(send, 'pts', pairs)  6.14 us
    pallas_call x1, Pallas kernels, gram_sums(): pl.pallas_call(gram_body, out_shape=(half, half), in_specs=[vmem] * 4, ou...  2.9 us
    convert_element_type x1, other arithmetic, dft_columns(): cosine = (scaled * jnp.cos(angles)).astype(jnp.bfloat16)  2.51 us
    pallas_call x1, Pallas kernels, scatter_points(): pl.pallas_call(scatter_body, out_shape=jax.ShapeDtypeStruct((points // 8,...  2.3 us
  transfers between devices with their start and end apart: 2, of which 2 were waited for; matrix products, arithmetic and copies ran while one was open for 4% of the time, Pallas kernels for 0%

profile of v5, /device:TPU:1, one launch (start us, length us, event | category | flops | bytes accessed | tf_op | source)
XLA Modules:
  0.0 71.8 jit_solution(13937258047410452297)
XLA Ops:
  0.0 0.0 copy-start
  0.0 2.3 %scatter_points.1 = bf16[32,16,640]{2,1,0:T(8,128)(2,1)} custom-call(bf16[16,5,16,256]{3,2,1,0:T(8,128)(2,1)} %bitcast.8), custom_call_target="tpu_custom_call" | custom-call | tf_op jit(solution)/shard_map/scatter_points/pallas_call | solution.py:99
  2.3 12.5 %all-to-all-start = ((bf16[32,16,640]{2,1,0:T(8,128)(2,1)}), bf16[32,16,640]{2,1,0:T(8,128)(2,1)S(1)}, u32[]{:S(2)}, u32[]{:S(2)}) async-start(bf16[32,16,640]{2,1,0:T(8,128)(2,1)} %scatter_points.1), calls=%async_computation | async-start | bytes 1310720 | tf_op jit(solution)/shard_map/all_to_all | solution.py:21
  14.8 0.0 copy-start.2
  14.8 0.0 copy-done
  14.8 0.1 constant_dynamic-slice_fusion
  14.9 0.1 broadcast_in_dim.6
  15.0 0.4 copy-done.2
  15.5 0.2 convert_reduce_fusion
  15.7 0.0 copy-start.3
  15.7 0.7 copy-done.3
  16.3 2.5 %multiply_convert_fusion.1 = (bf16[512,256]{1,0:T(8,128)(2,1)S(1)}, bf16[512,256]{1,0:T(8,128)(2,1)S(1)}) fusion(s32[512]{0:T(512)S(1)} %add_select_fusion.1, s32[256]{0:T(256)S(1)} %copy-done.3, f32[512]{0:T(512)S(1)} %get-tuple-element.11, f32[512]{0:T(512)S(1)} %get-tuple-element.12), kind=kLoop, calls=%fused_computation.11 | loop fusion | flops 2359296 | bytes 531456 | tf_op jit(solution)/shard_map/convert_element_type | solution.py:32
  18.9 0.1 fusion.3.slot_ref
  19.0 7.4 %all-to-all-done.x_ref = bf16[32,16,640]{2,1,0:T(8,128)(2,1)S(1)} async-done(((bf16[32,16,640]{2,1,0:T(8,128)(2,1)}), bf16[32,16,640]{2,1,0:T(8,128)(2,1)S(1)}, u32[]{:S(2)}, u32[]{:S(2)}) %all-to-all-start) | async-done | bytes 655392 | tf_op jit(solution)/shard_map/all_to_all | solution.py:21
  26.4 0.1 broadcast_in_dim.7.w_ref
  26.5 2.9 %gram_sums.1 = (f32[256,256]{1,0:T(8,128)S(1)}, f32[256,256]{1,0:T(8,128)S(1)}) custom-call(bf16[32,16,640]{2,1,0:T(8,128)(2,1)S(1)} %all-to-all-done.x_ref, bf16[512,512]{1,0:T(8,128)(2,1)S(1)} %pad_maximum_fusion.table_ref, f32[40,128]{1,0:T(8,128)S(1)} %broadcast_in_dim.7.w_ref, bf16[512,256]{1,0:T(8,128)(2,1)S(1)} %fusion.3.slot_ref), custom_call_target="tpu_custom_call" | custom-call | tf_op jit(solution)/shard_map/gram_sums/pallas_call | solution.py:185
  29.4 6.1 %collective-permute-start = (f32[256,256]{1,0:T(8,128)S(1)}, f32[256,256]{1,0:T(8,128)S(1)}, u32[]{:S(2)}, u32[]{:S(2)}) collective-permute-start(f32[256,256]{1,0:T(8,128)S(1)} %get-tuple-element.8), channel_id=1, source_target_pairs={{0,1},{1,0},{2,3},{3,2},{4,5},{5,4},{6,7},{7,6},{8,9},{9,8},{10,11... | collective-permute-start | bytes 786440 | tf_op jit(solution)/shard_map/ppermute | solution.py:236
  35.5 1.1 %collective-permute-done = f32[256,256]{1,0:T(8,128)S(1)} collective-permute-done((f32[256,256]{1,0:T(8,128)S(1)}, f32[256,256]{1,0:T(8,128)S(1)}, u32[]{:S(2)}, u32[]{:S(2)}) %collective-permute-start) | collective-permute-done | bytes 262176 | tf_op jit(solution)/shard_map/ppermute | solution.py:236
  36.7 15.9 %all_to_all.15 = f32[32,8,256]{2,1,0:T(8,128)S(1)} all-to-all(f32[32,8,256]{2,1,0:T(8,128)S(1)} %add_bitcast_fusion), channel_id=1, replica_groups={{288,304,320,336,352,368,384,400,416,432,448,464,480,496,0,16,32,48,64,..., dimensions={0} | all-to-all | bytes 524288 | tf_op jit(solution)/shard_map/all_to_all | solution.py:21
  52.6 0.0 copy-start.1
  52.7 18.1 %all_to_all.16 = f32[16,8,256]{2,1,0:T(8,128)S(1)} all-to-all(f32[16,8,256]{2,1,0:T(8,128)S(1)} %broadcast_in_dim.8), channel_id=1, replica_groups={{12,13,14,15,0,1,2,3,4,5,6,7,8,9,10,11},{28,29,30,31,16,17,18,19,20,21,..., dimensions={0} | all-to-all | bytes 262144 | tf_op jit(solution)/shard_map/all_to_all | solution.py:21
  70.8 0.0 copy-done.1
  70.8 1.0 %fusion.11 = f32[16,512]{1,0:T(8,128)} fusion(f32[16,256]{1,0:T(8,128)S(1)} %bitcast_reduce_fusion, f32[256,512]{1,0:T(8,128)S(1)} %copy-done.1), kind=kOutput, calls=%fused_computation.38 | convolution fusion | flops 25165824 | bytes 573440 | tf_op jit(solution)/shard_map/dot_general | solution.py:242
  (8 shorter events, 0.2 us)
Async XLA Ops:
  0.0 14.8 %copy-start = (f32[5,256]{1,0:T(8,128)S(1)}, f32[5,256]{1,0:T(8,128)}, u32[]{:S(2)}) copy-start(f32[5,256]{1,0:T(8,128)} %param.6) | copy-start | bytes 15364
  2.3 24.1 %all-to-all-start = ((bf16[32,16,640]{2,1,0:T(8,128)(2,1)}), bf16[32,16,640]{2,1,0:T(8,128)(2,1)S(1)}, u32[]{:S(2)}, u32[]{:S(2)}) async-start(bf16[32,16,640]{2,1,0:T(8,128)(2,1)} %scatter_points.1), calls=%async_computation | async-start | bytes 1310720 | tf_op jit(solution)/shard_map/all_to_all | solution.py:21
  14.8 0.7 copy-start.2
  15.7 0.7 copy-start.3
  29.4 7.3 %collective-permute-start = (f32[256,256]{1,0:T(8,128)S(1)}, f32[256,256]{1,0:T(8,128)S(1)}, u32[]{:S(2)}, u32[]{:S(2)}) collective-permute-start(f32[256,256]{1,0:T(8,128)S(1)} %get-tuple-element.8), channel_id=1, source_target_pairs={{0,1},{1,0},{2,3},{3,2},{4,5},{5,4},{6,7},{7,6},{8,9},{9,8},{10,11... | collective-permute-start | bytes 786440 | tf_op jit(solution)/shard_map/ppermute | solution.py:236
  52.6 18.2 %copy-start.1 = (f32[256,512]{1,0:T(8,128)S(1)}, f32[256,512]{1,0:T(8,128)}, u32[]{:S(2)}) copy-start(f32[256,512]{1,0:T(8,128)} %constant.103.clone) | copy-start | bytes 1572868

commit v6 on v5

--- a/solution.py
+++ b/solution.py
@@ -199,6 +199,30 @@
     )(by_point, table, row_weights, slots)
 
 
+def finish_body(parts_ref, unpack_ref, out_ref):
+    total = jnp.sum(parts_ref[...], axis=0)
+    first = total.astype(jnp.bfloat16)
+    rest = total - first.astype(jnp.float32)
+    second = rest.astype(jnp.bfloat16)
+    third = (rest - second.astype(jnp.float32)).astype(jnp.bfloat16)
+    rows = jnp.concatenate([first, second, third], axis=0)
+    full = jnp.dot(rows, unpack_ref[...], preferred_element_type=jnp.float32)
+    slots = total.shape[0]
+    out_ref[...] = full[:slots] + full[slots : 2 * slots] + full[2 * slots :]
+
+
+def finish(parts, unpack):
+    vmem = pl.BlockSpec(memory_space=pltpu.VMEM)
+    return pl.pallas_call(
+        finish_body,
+        out_shape=jax.ShapeDtypeStruct((parts.shape[1], unpack.shape[1]), jnp.float32),
+        in_specs=[vmem] * 2,
+        out_specs=vmem,
+        compiler_params=pltpu.CompilerParams(vmem_limit_bytes=8 * 1024 * 1024),
+        name="finish",
+    )(parts, unpack)
+
+
 def unpack_matrix(blocks):
     table = np.zeros((256, 2 * blocks * blocks), np.float32)
     half = blocks // 2
@@ -238,10 +262,8 @@
     owned = jnp.sum(partial, axis=0)
     copies = jnp.broadcast_to(owned[None], (pts_count,) + owned.shape)
     copies = exchange(copies, "pts", FIRST_SUMS)
-    summed = jnp.sum(copies.reshape(pts_count // 2, CAP, 256), axis=0)
-    return jnp.dot(
-        summed, jnp.asarray(unpack_matrix(blocks)), precision=lax.Precision.HIGHEST
-    )
+    parts = copies.reshape(pts_count // 2, CAP, 256)
+    return finish(parts, jnp.asarray(unpack_matrix(blocks), jnp.bfloat16))
 
 
 def solution(mesh):

time: 72.1 us -> 71.9 us (level)
  matrix products: 0.99 us -> 0 us
  Pallas kernels: 5.19 us -> 5.94 us
    dot_general x1 -> x0, matrix products: 0.99 us -> none  [shards(): jnp.dot(summed, jnp.asarray(unpack_matrix(blocks)), precision=lax.Precisi...]
    pallas_call x0 -> x1, Pallas kernels: none -> 0.78 us  [finish(): pl.pallas_call(finish_body, out_shape=jax.ShapeDtypeStruct((parts.shape[1...]
where the time goes in v6:
time: 71.9 us; the launch traced here: 71.5 us
  blocking collectives  34 us (47%)
  starting transfers between devices  18.6 us (26%)
  waiting for transfers between devices  8.54 us (12%)
  Pallas kernels  5.94 us (8%)
  other arithmetic  2.93 us (4%)
  local copies, waits for them, and re-layouts  1.38 us (2%)
    all_to_all x2, blocking collectives, exchange(): lax.all_to_all(value, axis, split_axis=0, concat_axis=0, tiled=True, axis...  34 us
    all_to_all x1, starting transfers between devices, exchange(): lax.all_to_all(value, axis, split_axis=0, concat_axis=0, tiled=True, axis...  12.5 us
    all_to_all x1, waiting for transfers between devices, exchange(): lax.all_to_all(value, axis, split_axis=0, concat_axis=0, tiled=True, axis...  7.4 us
    ppermute x1, starting transfers between devices, shards(): lax.ppermute(send, 'pts', pairs)  6.15 us
    pallas_call x1, Pallas kernels, gram_sums(): pl.pallas_call(gram_body, out_shape=(half, half), in_specs=[vmem] * 4, ou...  2.9 us
    convert_element_type x1, other arithmetic, dft_columns(): cosine = (scaled * jnp.cos(angles)).astype(jnp.bfloat16)  2.51 us
    pallas_call x1, Pallas kernels, scatter_points(): pl.pallas_call(scatter_body, out_shape=jax.ShapeDtypeStruct((points // 8,...  2.26 us
  transfers between devices with their start and end apart: 2, of which 2 were waited for; matrix products, arithmetic and copies ran while one was open for 4% of the time, Pallas kernels for 0%

profile of v6, /device:TPU:1, one launch (start us, length us, event | category | flops | bytes accessed | tf_op | source)
XLA Modules:
  0.0 71.5 jit_solution(3140782685588245355)
XLA Ops:
  0.0 0.0 copy-start
  0.0 2.3 %scatter_points.1 = bf16[32,16,640]{2,1,0:T(8,128)(2,1)} custom-call(bf16[16,5,16,256]{3,2,1,0:T(8,128)(2,1)} %bitcast.5), custom_call_target="tpu_custom_call" | custom-call | tf_op jit(solution)/shard_map/scatter_points/pallas_call | solution.py:99
  2.3 12.5 %all-to-all-start = ((bf16[32,16,640]{2,1,0:T(8,128)(2,1)}), bf16[32,16,640]{2,1,0:T(8,128)(2,1)S(1)}, u32[]{:S(2)}, u32[]{:S(2)}) async-start(bf16[32,16,640]{2,1,0:T(8,128)(2,1)} %scatter_points.1), calls=%async_computation | async-start | bytes 1310720 | tf_op jit(solution)/shard_map/all_to_all | solution.py:21
  14.8 0.0 copy-start.2
  14.8 0.0 copy-done
  14.8 0.1 constant_dynamic-slice_fusion
  14.9 0.1 broadcast_in_dim.6
  15.0 0.4 copy-done.2
  15.4 0.2 convert_reduce_fusion
  15.6 0.0 copy-start.3
  15.6 0.7 copy-done.3
  16.3 2.5 %multiply_convert_fusion.1 = (bf16[512,256]{1,0:T(8,128)(2,1)S(1)}, bf16[512,256]{1,0:T(8,128)(2,1)S(1)}) fusion(s32[512]{0:T(512)S(1)} %add_select_fusion.1, s32[256]{0:T(256)S(1)} %copy-done.3, f32[512]{0:T(512)S(1)} %get-tuple-element.11, f32[512]{0:T(512)S(1)} %get-tuple-element.12), kind=kLoop, calls=%fused_computation.11 | loop fusion | flops 2359296 | bytes 531456 | tf_op jit(solution)/shard_map/convert_element_type | solution.py:32
  18.9 0.1 fusion.3.slot_ref
  19.0 7.4 %all-to-all-done.x_ref = bf16[32,16,640]{2,1,0:T(8,128)(2,1)S(1)} async-done(((bf16[32,16,640]{2,1,0:T(8,128)(2,1)}), bf16[32,16,640]{2,1,0:T(8,128)(2,1)S(1)}, u32[]{:S(2)}, u32[]{:S(2)}) %all-to-all-start) | async-done | bytes 655392 | tf_op jit(solution)/shard_map/all_to_all | solution.py:21
  26.4 0.1 broadcast_in_dim.7.w_ref
  26.4 2.9 %gram_sums.1 = (f32[256,256]{1,0:T(8,128)S(1)}, f32[256,256]{1,0:T(8,128)S(1)}) custom-call(bf16[32,16,640]{2,1,0:T(8,128)(2,1)S(1)} %all-to-all-done.x_ref, bf16[512,512]{1,0:T(8,128)(2,1)S(1)} %pad_maximum_fusion.table_ref, f32[40,128]{1,0:T(8,128)S(1)} %broadcast_in_dim.7.w_ref, bf16[512,256]{1,0:T(8,128)(2,1)S(1)} %fusion.3.slot_ref), custom_call_target="tpu_custom_call" | custom-call | tf_op jit(solution)/shard_map/gram_sums/pallas_call | solution.py:185
  29.4 6.1 %collective-permute-start = (f32[256,256]{1,0:T(8,128)S(1)}, f32[256,256]{1,0:T(8,128)S(1)}, u32[]{:S(2)}, u32[]{:S(2)}) collective-permute-start(f32[256,256]{1,0:T(8,128)S(1)} %get-tuple-element.8), channel_id=1, source_target_pairs={{0,1},{1,0},{2,3},{3,2},{4,5},{5,4},{6,7},{7,6},{8,9},{9,8},{10,11... | collective-permute-start | bytes 786440 | tf_op jit(solution)/shard_map/ppermute | solution.py:260
  35.5 1.1 %collective-permute-done = f32[256,256]{1,0:T(8,128)S(1)} collective-permute-done((f32[256,256]{1,0:T(8,128)S(1)}, f32[256,256]{1,0:T(8,128)S(1)}, u32[]{:S(2)}, u32[]{:S(2)}) %collective-permute-start) | collective-permute-done | bytes 262176 | tf_op jit(solution)/shard_map/ppermute | solution.py:260
  36.7 15.9 %all_to_all.15 = f32[32,8,256]{2,1,0:T(8,128)S(1)} all-to-all(f32[32,8,256]{2,1,0:T(8,128)S(1)} %add_bitcast_fusion), channel_id=1, replica_groups={{288,304,320,336,352,368,384,400,416,432,448,464,480,496,0,16,32,48,64,..., dimensions={0} | all-to-all | bytes 524288 | tf_op jit(solution)/shard_map/all_to_all | solution.py:21
  52.6 0.0 copy-start.1
  52.6 18.1 %all_to_all.16 = f32[16,8,256]{2,1,0:T(8,128)S(1)} all-to-all(f32[16,8,256]{2,1,0:T(8,128)S(1)} %broadcast_in_dim.8), channel_id=1, replica_groups={{12,13,14,15,0,1,2,3,4,5,6,7,8,9,10,11},{28,29,30,31,16,17,18,19,20,21,..., dimensions={0} | all-to-all | bytes 262144 | tf_op jit(solution)/shard_map/all_to_all | solution.py:21
  70.7 0.0 copy-done.1
  70.7 0.8 %finish.1 = f32[16,512]{1,0:T(8,128)} custom-call(f32[8,16,256]{2,1,0:T(8,128)S(1)} %bitcast.4, bf16[256,512]{1,0:T(8,128)(2,1)S(1)} %copy-done.1), custom_call_target="tpu_custom_call" | custom-call | tf_op jit(solution)/shard_map/finish/pallas_call | solution.py:216
  (7 shorter events, 0.2 us)
Async XLA Ops:
  0.0 14.8 %copy-start = (f32[5,256]{1,0:T(8,128)S(1)}, f32[5,256]{1,0:T(8,128)}, u32[]{:S(2)}) copy-start(f32[5,256]{1,0:T(8,128)} %param.6) | copy-start | bytes 15364
  2.3 24.1 %all-to-all-start = ((bf16[32,16,640]{2,1,0:T(8,128)(2,1)}), bf16[32,16,640]{2,1,0:T(8,128)(2,1)S(1)}, u32[]{:S(2)}, u32[]{:S(2)}) async-start(bf16[32,16,640]{2,1,0:T(8,128)(2,1)} %scatter_points.1), calls=%async_computation | async-start | bytes 1310720 | tf_op jit(solution)/shard_map/all_to_all | solution.py:21
  14.8 0.7 copy-start.2
  15.6 0.7 copy-start.3
  29.4 7.3 %collective-permute-start = (f32[256,256]{1,0:T(8,128)S(1)}, f32[256,256]{1,0:T(8,128)S(1)}, u32[]{:S(2)}, u32[]{:S(2)}) collective-permute-start(f32[256,256]{1,0:T(8,128)S(1)} %get-tuple-element.8), channel_id=1, source_target_pairs={{0,1},{1,0},{2,3},{3,2},{4,5},{5,4},{6,7},{7,6},{8,9},{9,8},{10,11... | collective-permute-start | bytes 786440 | tf_op jit(solution)/shard_map/ppermute | solution.py:260
  52.6 18.1 %copy-start.1 = (bf16[256,512]{1,0:T(8,128)(2,1)S(1)}, bf16[256,512]{1,0:T(8,128)(2,1)}, u32[]{:S(2)}) copy-start(bf16[256,512]{1,0:T(8,128)(2,1)} %constant.103.clone.unpack_ref) | copy-start | bytes 786436

commit v7 on v6

--- a/solution.py
+++ b/solution.py
@@ -12,7 +12,7 @@
 LANES = 128
 FIRST_POINTS = 18
 FIRST_SLOTS = 18
-FIRST_SUMS = 12
+FIRST_SUMS = 10
 
 
 def exchange(value, axis, first):

time: 71.9 us -> 72 us (level)
  no operation moved by 1% of the time
where the time goes in v7:
time: 72 us; the launch traced here: 71.7 us
  blocking collectives  34.2 us (48%)
  starting transfers between devices  18.6 us (26%)
  waiting for transfers between devices  8.54 us (12%)
  Pallas kernels  5.94 us (8%)
  other arithmetic  2.93 us (4%)
  local copies, waits for them, and re-layouts  1.38 us (2%)
    all_to_all x2, blocking collectives, exchange(): lax.all_to_all(value, axis, split_axis=0, concat_axis=0, tiled=True, axis...  34.2 us
    all_to_all x1, starting transfers between devices, exchange(): lax.all_to_all(value, axis, split_axis=0, concat_axis=0, tiled=True, axis...  12.5 us
    all_to_all x1, waiting for transfers between devices, exchange(): lax.all_to_all(value, axis, split_axis=0, concat_axis=0, tiled=True, axis...  7.4 us
    ppermute x1, starting transfers between devices, shards(): lax.ppermute(send, 'pts', pairs)  6.15 us
    pallas_call x1, Pallas kernels, gram_sums(): pl.pallas_call(gram_body, out_shape=(half, half), in_specs=[vmem] * 4, ou...  2.9 us
    convert_element_type x1, other arithmetic, dft_columns(): cosine = (scaled * jnp.cos(angles)).astype(jnp.bfloat16)  2.51 us
    pallas_call x1, Pallas kernels, scatter_points(): pl.pallas_call(scatter_body, out_shape=jax.ShapeDtypeStruct((points // 8,...  2.26 us
  transfers between devices with their start and end apart: 2, of which 2 were waited for; matrix products, arithmetic and copies ran while one was open for 4% of the time, Pallas kernels for 0%

profile of v7, /device:TPU:1, one launch (start us, length us, event | category | flops | bytes accessed | tf_op | source)
XLA Modules:
  0.0 71.7 jit_solution(703742589167677511)
XLA Ops:
  0.0 0.0 copy-start
  0.0 2.3 %scatter_points.1 = bf16[32,16,640]{2,1,0:T(8,128)(2,1)} custom-call(bf16[16,5,16,256]{3,2,1,0:T(8,128)(2,1)} %bitcast.5), custom_call_target="tpu_custom_call" | custom-call | tf_op jit(solution)/shard_map/scatter_points/pallas_call | solution.py:99
  2.3 12.5 %all-to-all-start = ((bf16[32,16,640]{2,1,0:T(8,128)(2,1)}), bf16[32,16,640]{2,1,0:T(8,128)(2,1)S(1)}, u32[]{:S(2)}, u32[]{:S(2)}) async-start(bf16[32,16,640]{2,1,0:T(8,128)(2,1)} %scatter_points.1), calls=%async_computation | async-start | bytes 1310720 | tf_op jit(solution)/shard_map/all_to_all | solution.py:21
  14.8 0.0 copy-start.2
  14.8 0.0 copy-done
  14.8 0.1 constant_dynamic-slice_fusion
  14.9 0.1 broadcast_in_dim.6
  15.0 0.4 copy-done.2
  15.4 0.2 convert_reduce_fusion
  15.6 0.0 copy-start.3
  15.6 0.7 copy-done.3
  16.3 2.5 %multiply_convert_fusion.1 = (bf16[512,256]{1,0:T(8,128)(2,1)S(1)}, bf16[512,256]{1,0:T(8,128)(2,1)S(1)}) fusion(s32[512]{0:T(512)S(1)} %add_select_fusion.1, s32[256]{0:T(256)S(1)} %copy-done.3, f32[512]{0:T(512)S(1)} %get-tuple-element.11, f32[512]{0:T(512)S(1)} %get-tuple-element.12), kind=kLoop, calls=%fused_computation.11 | loop fusion | flops 2359296 | bytes 531456 | tf_op jit(solution)/shard_map/convert_element_type | solution.py:32
  18.9 0.1 fusion.3.slot_ref
  19.0 7.4 %all-to-all-done.x_ref = bf16[32,16,640]{2,1,0:T(8,128)(2,1)S(1)} async-done(((bf16[32,16,640]{2,1,0:T(8,128)(2,1)}), bf16[32,16,640]{2,1,0:T(8,128)(2,1)S(1)}, u32[]{:S(2)}, u32[]{:S(2)}) %all-to-all-start) | async-done | bytes 655392 | tf_op jit(solution)/shard_map/all_to_all | solution.py:21
  26.4 0.1 broadcast_in_dim.7.w_ref
  26.4 2.9 %gram_sums.1 = (f32[256,256]{1,0:T(8,128)S(1)}, f32[256,256]{1,0:T(8,128)S(1)}) custom-call(bf16[32,16,640]{2,1,0:T(8,128)(2,1)S(1)} %all-to-all-done.x_ref, bf16[512,512]{1,0:T(8,128)(2,1)S(1)} %pad_maximum_fusion.table_ref, f32[40,128]{1,0:T(8,128)S(1)} %broadcast_in_dim.7.w_ref, bf16[512,256]{1,0:T(8,128)(2,1)S(1)} %fusion.3.slot_ref), custom_call_target="tpu_custom_call" | custom-call | tf_op jit(solution)/shard_map/gram_sums/pallas_call | solution.py:185
  29.4 6.1 %collective-permute-start = (f32[256,256]{1,0:T(8,128)S(1)}, f32[256,256]{1,0:T(8,128)S(1)}, u32[]{:S(2)}, u32[]{:S(2)}) collective-permute-start(f32[256,256]{1,0:T(8,128)S(1)} %get-tuple-element.8), channel_id=1, source_target_pairs={{0,1},{1,0},{2,3},{3,2},{4,5},{5,4},{6,7},{7,6},{8,9},{9,8},{10,11... | collective-permute-start | bytes 786440 | tf_op jit(solution)/shard_map/ppermute | solution.py:260
  35.5 1.1 %collective-permute-done = f32[256,256]{1,0:T(8,128)S(1)} collective-permute-done((f32[256,256]{1,0:T(8,128)S(1)}, f32[256,256]{1,0:T(8,128)S(1)}, u32[]{:S(2)}, u32[]{:S(2)}) %collective-permute-start) | collective-permute-done | bytes 262176 | tf_op jit(solution)/shard_map/ppermute | solution.py:260
  36.7 15.9 %all_to_all.15 = f32[32,8,256]{2,1,0:T(8,128)S(1)} all-to-all(f32[32,8,256]{2,1,0:T(8,128)S(1)} %add_bitcast_fusion), channel_id=1, replica_groups={{288,304,320,336,352,368,384,400,416,432,448,464,480,496,0,16,32,48,64,..., dimensions={0} | all-to-all | bytes 524288 | tf_op jit(solution)/shard_map/all_to_all | solution.py:21
  52.6 0.0 copy-start.1
  52.6 18.3 %all_to_all.16 = f32[16,8,256]{2,1,0:T(8,128)S(1)} all-to-all(f32[16,8,256]{2,1,0:T(8,128)S(1)} %broadcast_in_dim.8), channel_id=1, replica_groups={{10,11,12,13,14,15,0,1,2,3,4,5,6,7,8,9},{26,27,28,29,30,31,16,17,18,19,..., dimensions={0} | all-to-all | bytes 262144 | tf_op jit(solution)/shard_map/all_to_all | solution.py:21
  70.9 0.0 copy-done.1
  70.9 0.8 %finish.1 = f32[16,512]{1,0:T(8,128)} custom-call(f32[8,16,256]{2,1,0:T(8,128)S(1)} %bitcast.4, bf16[256,512]{1,0:T(8,128)(2,1)S(1)} %copy-done.1), custom_call_target="tpu_custom_call" | custom-call | tf_op jit(solution)/shard_map/finish/pallas_call | solution.py:216
  (7 shorter events, 0.2 us)
Async XLA Ops:
  0.0 14.8 %copy-start = (f32[5,256]{1,0:T(8,128)S(1)}, f32[5,256]{1,0:T(8,128)}, u32[]{:S(2)}) copy-start(f32[5,256]{1,0:T(8,128)} %param.6) | copy-start | bytes 15364
  2.3 24.1 %all-to-all-start = ((bf16[32,16,640]{2,1,0:T(8,128)(2,1)}), bf16[32,16,640]{2,1,0:T(8,128)(2,1)S(1)}, u32[]{:S(2)}, u32[]{:S(2)}) async-start(bf16[32,16,640]{2,1,0:T(8,128)(2,1)} %scatter_points.1), calls=%async_computation | async-start | bytes 1310720 | tf_op jit(solution)/shard_map/all_to_all | solution.py:21
  14.8 0.7 copy-start.2
  15.6 0.7 copy-start.3
  29.4 7.3 %collective-permute-start = (f32[256,256]{1,0:T(8,128)S(1)}, f32[256,256]{1,0:T(8,128)S(1)}, u32[]{:S(2)}, u32[]{:S(2)}) collective-permute-start(f32[256,256]{1,0:T(8,128)S(1)} %get-tuple-element.8), channel_id=1, source_target_pairs={{0,1},{1,0},{2,3},{3,2},{4,5},{5,4},{6,7},{7,6},{8,9},{9,8},{10,11... | collective-permute-start | bytes 786440 | tf_op jit(solution)/shard_map/ppermute | solution.py:260
  52.6 18.3 %copy-start.1 = (bf16[256,512]{1,0:T(8,128)(2,1)S(1)}, bf16[256,512]{1,0:T(8,128)(2,1)}, u32[]{:S(2)}) copy-start(bf16[256,512]{1,0:T(8,128)(2,1)} %constant.103.clone.unpack_ref) | copy-start | bytes 786436
